TPU v7x, 512 devices: a whole 4x4x16 slice. The times are simulated.
512 devices in a mesh: gx: 16 (over z_lo, core), gy: 8 (over z_hi, x), gz: 4 (over y).
Axes of the slice: x: 4, y: 4, z: 16 (z_hi: 2, z_lo: 8; z = z_hi * 8 + z_lo), core: 2. Of those that a mesh axis runs over, the one named last changes fastest.
Arguments:
- magnetization: float32 [3, 64, 1024, 1024], P(None, 'gz', 'gx', 'gy'), may hold values from -6 to 6
- stiffness: float32 [64, 1024, 1024], P('gz', 'gx', 'gy'), may hold values from 0.02 to 0.2
- residual_top: float32 [1024, 1024], P('gx', ('gy', 'gz')), may hold values from -6 to 6
- residual_side: float32 [1024, 64], P('gy', 'gz'), may hold values from -6 to 6
- top_kernel: float32 [2, 2, 2048, 2048], P(None, None, ('gx', 'gy', 'gz')), may hold values from -6 to 6
- side_kernel: float32 [2, 2, 128, 2048], P(None, None, ('gy', 'gz')), may hold values from -6 to 6
Outputs:
- gradient: float32 [3, 64, 1024, 1024], P(None, 'gz', 'gx', 'gy')
All inputs are finite; a program needn't handle non-finite values.
Results may differ from a plain program's by a relative error of at most 0.0001.
Values sent between devices are 32-bit elements; how exact they have to be, the bound alone decides.
A program may use at most 64 MiB of HBM per device.

v0:
```python
import math

import jax
import jax.numpy as jnp
import numpy as np
from jax import lax
from jax.experimental import pallas as pl
from jax.experimental.pallas import tpu as pltpu
from jax.sharding import PartitionSpec as P

F32 = jnp.float32
MESH = pl.DeviceIdType.MESH
TOP_SCALE = 1.0 / 2048.0**2
SIDE_SCALE = 1.0 / (2048.0 * 128.0)


def _dot(a, b, ca=1, cb=0):
    return lax.dot_general(
        a, b, (((ca,), (cb,)), ((), ())), precision=lax.Precision.HIGHEST, preferred_element_type=F32
    )


def _cs(first, second, modulus):
    angle = 2.0 * np.pi * ((first * second) % modulus) / modulus
    return np.cos(angle), np.sin(angle)


def const_tables():
    i = np.arange
    c, s = _cs(i(16)[:, None], i(128)[None, :], 32)
    gl16 = np.concatenate([c, s], 1)
    gl32 = np.repeat(gl16, 2, axis=0)
    c, s = _cs(i(64)[:, None], i(128)[None, :], 2048)
    twist = np.concatenate([c, s], 0)
    c, s = _cs(i(16)[:, None], i(64)[None, :], 16)
    fwd = np.block([[c, s], [-s, c]])
    inv = np.block([[c.T, -s.T], [s.T, c.T]])
    back = gl16.reshape(16, 2, 128).transpose(1, 0, 2).reshape(32, 128)
    c, s = _cs(i(32)[:, None], i(32)[None, :], 32)
    fold = np.concatenate([c, s], 0)
    return [np.asarray(t, np.float32) for t in (gl32, gl16, twist, fwd, inv, back, fold)]


def _iota(shape, dim):
    return lax.broadcasted_iota(jnp.int32, shape, dim)


def _angle(product, modulus):
    return (product & (modulus - 1)).astype(F32) * (2.0 * math.pi / modulus)


def first_table(zh, n0):
    row = _iota((128, 256), 0)
    col = _iota((128, 256), 1)
    ky = 64 * (row // 4) + row % 4 + 4 * n0
    y = 32 * (col // 16) + col % 16 + 512 * zh
    parts = []
    for h in (0, 1):
        t = _angle(ky * (y + 16 * h), 2048)
        parts += [jnp.cos(t), -jnp.sin(t)]
    return parts


def last_table(zh, n0):
    row = _iota((16, 64), 0)
    col = _iota((16, 64), 1)
    s = 4 * (col % 16) + col // 16
    out = []
    for a in (0, 1):
        t = _angle(s * (32 * row + n0 + 16 * a + 512 * zh), 2048)
        out.append(jnp.concatenate([jnp.cos(t) * TOP_SCALE, jnp.sin(t) * TOP_SCALE], 0))
    return out


def side_table(zh, n0):
    row = _iota((16, 64), 0)
    z = _iota((16, 64), 1)
    own = jnp.where(row < 8, zh, 1 - zh)
    t = _angle((64 * own + 4 * n0 + row % 4) * z, 128)
    return jnp.where(row % 8 < 4, jnp.cos(t), -jnp.sin(t))


def side_last_table(yy):
    row = _iota((16, 128), 0)
    col = _iota((16, 128), 1)
    kz = 64 * (col % 2) + 4 * ((col // 2) % 16) + col // 32
    t = _angle(kz * (row + 16 * yy), 128)
    return jnp.concatenate([jnp.cos(t) * SIDE_SCALE, jnp.sin(t) * SIDE_SCALE], 0)


def first_stage(w, packed, roll):
    p = [_dot(t, packed) for t in w]
    low = _iota((128, 128), 1) < 64
    return jnp.where(low, p[0] + roll(p[2], 64), roll(p[1], 64) + p[3])


def side_first(w, data, roll):
    t = _dot(w, data)
    low = _iota((4, 128), 1) < 64
    own, other = [], []
    for x in range(4):
        for base, out in ((0, own), (8, other)):
            o = t[base : base + 8, 128 * x : 128 * x + 128]
            q = roll(o, 64)
            f0 = jnp.where(low, o[0:4], q[4:8])
            f1 = jnp.where(low, q[0:4], o[4:8])
            out.append(jnp.concatenate([f0, f1], 0))
    return own, other


def line_stage(rows, kernel_at, tabs, roll):
    gl, twist, fwd, inv, back = tabs
    twc, tws = twist[:64], twist[64:]
    p = _dot(jnp.concatenate(rows, 1), gl, 0, 0)
    mid = []
    for r in range(4):
        q = p[128 * r : 128 * r + 128]
        bre = q[:64, :128] + q[64:, 128:]
        bim = q[64:, :128] - q[:64, 128:]
        mid.append(jnp.concatenate([bre * twc + bim * tws, bim * twc - bre * tws], 0))
    spectrum = _dot(fwd, jnp.concatenate(mid, 1))
    weighted = []
    for c in range(2):
        for r in range(4):
            sre = spectrum[:16, 128 * r : 128 * r + 128]
            sim = spectrum[16:, 128 * r : 128 * r + 128]
            kre, kim = kernel_at(c, 0, r), kernel_at(c, 1, r)
            weighted.append(
                jnp.concatenate([kre * sre + kim * sim, kre * sim - kim * sre], 0)
            )
    v = _dot(inv, jnp.concatenate(weighted, 1))
    turned = []
    for cr in range(8):
        vre = v[:64, 128 * cr : 128 * cr + 128]
        vim = v[64:, 128 * cr : 128 * cr + 128]
        turned += [vre * twc - vim * tws, vim * twc + vre * tws]
    u = _dot(back, jnp.concatenate(turned, 0), 1, 1)
    return spread(u, 16, roll)


def spread(u, half, roll):
    sign = jnp.where(_iota((half, 128), 1) < 64, -1.0, 1.0)
    out = []
    for cr in range(8):
        lanes = slice(128 * cr, 128 * cr + 128)
        out.append(u[:half, lanes] + sign * roll(u[half:, lanes], 64))
    return out


def fold_stage(rows, fold, roll):
    return spread(_dot(fold, jnp.concatenate(rows, 1)), 32, roll)


def last_stage(table, rows, roll):
    g = _dot(table, jnp.concatenate(rows, 1))
    low = _iota((16, 128), 1) < 64
    part = [g[:16, 128 * c : 128 * c + 128] - roll(g[16:, 128 * c : 128 * c + 128], 64) for c in (0, 1)]
    return jnp.where(low, part[0], roll(part[1], 64))


def plane_id(zh, n):
    return {"gy": 4 * zh + n // 4, "gz": n % 4}


def ring_place(v):
    z = v // 2
    return 2 * (z % 8) + v % 2, z // 8


def rows8(start, size):
    return pl.ds(pl.multiple_of(start, 8), size)


def body(
    mag, stiff, rtop, rside, ktop, kside, gl32, gl16, twist, fwd, inv, back, fold,
    exch, top, side,
    field, kraw, kt, ks,
    send1, recv1, send2, recv2, send3, recv3, send4, recv4, send5, recv5,
    hop1, line1, own3, hop2, other3, recvs,
    hx_out_hi, hx_out_lo, hx_lo, hx_hi, hy_out_hi, hy_out_lo, hy_lo, hy_hi,
    local, ssem, rsem, hsend, hrecv,
):
    gx, gy, gz = lax.axis_index("gx"), lax.axis_index("gy"), lax.axis_index("gz")
    zh, xx = gy // 4, gy % 4
    n0 = 4 * xx + gz
    m0 = 2 * gx + zh
    v0 = 2 * (8 * zh + gx // 2) + gx % 2
    crosses = jnp.logical_or(gy == 3, gy == 4)
    far = {"gx": (gx + 8) % 16, "gy": 4 * (1 - zh) + xx}

    def roll(value, shift):
        return pltpu.roll(value, shift, 1)

    def over_plane(action):
        def step(k, carry):
            action((n0 + k) % 16)
            return carry

        lax.fori_loop(1, 16, step, 0)

    def over_column(action):
        def step(k, carry):
            half = (k + 1) // 2
            off = jnp.where(k % 2 == 1, 16 - half, 16 + half)
            px, ph = ring_place((v0 + off) % 32)
            action(2 * px + ph, {"gx": px, "gy": 4 * ph + xx})
            return carry

        lax.fori_loop(0, 31, step, 0)

    def remote(src, dst, sems, target):
        send_sem, recv_sem = sems
        return pltpu.make_async_remote_copy(
            src_ref=src, dst_ref=dst, send_sem=send_sem, recv_sem=recv_sem,
            device_id=target, device_id_type=MESH,
        )

    def wait_bytes(ref, sem):
        pltpu.make_async_copy(ref, ref, sem).wait()

    def pair(i):
        return ssem.at[i], rsem.at[i]

    loads = [
        pltpu.make_async_copy(mag, field.at[0:3, pl.ds(64, 1024)], local.at[0]),
        pltpu.make_async_copy(stiff, field.at[3:4, pl.ds(64, 1024)], local.at[1]),
        pltpu.make_async_copy(ktop, kraw.at[0], local.at[2]),
        pltpu.make_async_copy(kside, kraw.at[1], local.at[3]),
    ]
    for load in loads:
        load.start()
    barrier = pltpu.get_barrier_semaphore()
    over_plane(
        lambda n: pl.semaphore_signal(barrier, inc=1, device_id=plane_id(zh, n), device_id_type=MESH)
    )
    over_column(
        lambda m, target: pl.semaphore_signal(barrier, inc=1, device_id=target, device_id_type=MESH)
    )

    @pl.when(crosses)
    def _():
        pl.semaphore_signal(barrier, inc=1, device_id={"gy": 7 - gy}, device_id_type=MESH)

    send1[0:16, :] = jnp.concatenate([rtop[0:16, :], rtop[16:32, :]], 1)
    send1[16:32, :] = rside[...]
    recv1[rows8(32 * n0, 32), :] = send1[...]
    table1 = first_table(zh, n0)
    table_side = side_table(zh, n0)

    pl.semaphore_wait(barrier, 46 + crosses.astype(jnp.int32))

    over_plane(
        lambda n: remote(send1, recv1.at[rows8(32 * n0, 32)], pair(0), plane_id(zh, n)).start()
    )

    for load in loads:
        load.wait()
    zero_face = jnp.zeros((64, 128), F32)
    for c in range(4):
        hx_out_hi[16 * c : 16 * c + 16, :] = field[c, pl.ds(64 + 63, 16, stride=64), :]
        hx_out_lo[16 * c : 16 * c + 16, :] = field[c, pl.ds(64, 16, stride=64), :]
    lane = _iota((64, 128), 1)

    def pack(z, carry):
        hi, lo = carry
        for c in range(4):
            at = 16 * c + z
            turned = pltpu.roll(field[c, rows8(64 + 64 * z, 64), :], at + 1, 1)
            hi = jnp.where(lane == at, turned, hi)
            lo = jnp.where(lane == at + 1, turned, lo)
        return hi, lo

    packed_hi, packed_lo = lax.fori_loop(0, 16, pack, (zero_face, zero_face))
    hy_out_hi[...] = packed_hi
    hy_out_lo[...] = packed_lo

    x_up = (gx < 15, remote(hx_out_hi, hx_lo, (hsend.at[0], hrecv.at[0]), {"gx": (gx + 1) % 16}))
    x_dn = (gx > 0, remote(hx_out_lo, hx_hi, (hsend.at[1], hrecv.at[1]), {"gx": (gx + 15) % 16}))
    y_up = (gy < 7, remote(hy_out_hi, hy_lo, (hsend.at[2], hrecv.at[2]), {"gy": (gy + 1) % 8}))
    y_dn = (gy > 0, remote(hy_out_lo, hy_hi, (hsend.at[3], hrecv.at[3]), {"gy": (gy + 7) % 8}))
    z_up = (
        gz < 3,
        remote(field.at[:, pl.ds(1024, 64)], field.at[:, pl.ds(0, 64)],
               (hsend.at[4], hrecv.at[4]), {"gz": (gz + 1) % 4}),
    )
    z_dn = (
        gz > 0,
        remote(field.at[:, pl.ds(64, 64)], field.at[:, pl.ds(1088, 64)],
               (hsend.at[5], hrecv.at[5]), {"gz": (gz + 3) % 4}),
    )
    faces = (y_up, y_dn, z_up, z_dn, x_up, x_dn)
    for there, copy in faces:

        @pl.when(there)
        def _(copy=copy):
            copy.start()

    for missing, ref in ((gx == 0, hx_lo), (gx == 15, hx_hi), (gy == 0, hy_lo), (gy == 7, hy_hi)):

        @pl.when(missing)
        def _(ref=ref):
            ref[...] = zero_face

    for missing, start in ((gz == 0, 0), (gz == 3, 1088)):

        @pl.when(missing)
        def _(start=start):
            for c in range(4):
                field[c, pl.ds(start, 64), :] = zero_face

    for which, out in ((0, kt), (1, ks)):
        for cp in range(4):
            for j in range(16):
                out[pl.ds(64 * cp + j, 4, stride=16), :] = kraw[
                    which, cp // 2, cp % 2, :, 128 * j : 128 * j + 128
                ]

    wait_bytes(recv1.at[pl.ds(0, 480)], rsem.at[0])
    packed = jnp.concatenate([recv1[32 * n : 32 * n + 16, :] for n in range(16)], 0)
    first = first_stage(table1, packed, roll)
    for m in range(32):
        send2[m] = first[4 * m : 4 * m + 4]
    recv2[m0] = send2[m0]
    over_column(lambda m, target: remote(send2.at[m], recv2.at[m0], pair(1), target).start())

    data = jnp.concatenate(
        [
            jnp.concatenate(
                [recv1[32 * (4 * x + y) + 16 : 32 * (4 * x + y) + 32, :] for y in range(4)], 0
            )
            for x in range(4)
        ],
        1,
    )
    own, other = side_first(table_side, data, roll)
    for x in range(4):
        line1[rows8(32 * zh + 8 * x, 8), :] = own[x]
        hop1[8 * x : 8 * x + 8, :] = other[x]
    remote(hop1, line1.at[rows8(32 * zh, 32)], pair(5), far).start()

    table_last = last_table(zh, n0)
    table_side_last = side_last_table(gz)

    wait_bytes(recv2.at[pl.ds(0, 31)], rsem.at[1])
    shared = (twist[...], fwd[...], inv[...], back[...])
    lines = line_stage(
        [recv2[:, r, :] for r in range(4)],
        lambda c, p, r: kt[64 * (2 * c + p) + 16 * r : 64 * (2 * c + p) + 16 * r + 16, :],
        (gl32[...],) + shared,
        roll,
    )
    for cr in range(8):
        send3[pl.ds(cr, 16, stride=8), :] = lines[cr]
    recv3[rows8(8 * m0, 8), :] = send3[rows8(8 * gx, 8), :]
    over_column(
        lambda m, target: remote(
            send3.at[rows8(8 * (m // 2), 8)], recv3.at[rows8(8 * m0, 8)], pair(2), target
        ).start()
    )

    wait_bytes(line1.at[pl.ds(0, 32)], rsem.at[5])
    lines = line_stage(
        [line1[pl.ds(r, 16, stride=4), :] for r in range(4)],
        lambda c, p, r: ks[64 * (2 * c + p) + 16 * r : 64 * (2 * c + p) + 16 * r + 16, :],
        (gl16[...],) + shared,
        roll,
    )
    for cr in range(8):
        here, there = lines[cr][:8], lines[cr][8:]
        own3[pl.ds(cr, 8, stride=8), :] = jnp.where(zh == 0, here, there)
        hop2[pl.ds(cr, 8, stride=8), :] = jnp.where(zh == 0, there, here)
    remote(hop2, other3, pair(6), far).start()
    recvs[rows8(32 * n0 + 16 * zh, 16), :] = own3[rows8(16 * xx, 16), :]
    over_plane(
        lambda n: remote(
            own3.at[rows8(16 * (n // 4), 16)],
            recvs.at[rows8(32 * n0 + 16 * zh, 16)], pair(7), plane_id(zh, n),
        ).start()
    )

    arrivals = (
        (gx > 0, hx_lo, 0), (gx < 15, hx_hi, 1), (gy > 0, hy_lo, 2), (gy < 7, hy_hi, 3),
        (gz > 0, field.at[:, pl.ds(0, 64)], 4), (gz < 3, field.at[:, pl.ds(1088, 64)], 5),
    )
    for there, ref, i in arrivals:

        @pl.when(there)
        def _(ref=ref, i=i):
            wait_bytes(ref, hrecv.at[i])

    sub = _iota((64, 128), 0)

    def exchange(z, carry):
        def slab(c, step):
            return field[c, rows8(64 + 64 * (z + step), 64), :]

        def around(c):
            at = 16 * c + z
            center = slab(c, 0)
            below = jnp.where(sub == 0, hx_lo[pl.ds(at, 1), :], pltpu.roll(center, 1, 0))
            above = jnp.where(sub == 63, hx_hi[pl.ds(at, 1), :], pltpu.roll(center, 63, 0))
            left = jnp.where(lane == 0, pltpu.roll(hy_lo[...], 128 - at, 1), pltpu.roll(center, 1, 1))
            right = jnp.where(
                lane == 127, pltpu.roll(hy_hi[...], 126 - at, 1), pltpu.roll(center, 127, 1)
            )
            return center, (slab(c, -1), slab(c, 1), below, above, left, right)

        a, near = around(3)
        weights = [4.0 * a * b / (a + b) for b in near]
        for c in range(3):
            m, beside = around(c)
            total = weights[0] * (m - beside[0])
            for w, b in zip(weights[1:], beside[1:]):
                total = total + w * (m - b)
            exch[c, rows8(64 * z, 64), :] = total
        return carry

    lax.fori_loop(0, 16, exchange, 0)

    wait_bytes(other3, rsem.at[6])
    recvs[rows8(32 * n0 + 16 * (1 - zh), 16), :] = other3[rows8(16 * xx, 16), :]
    over_plane(
        lambda n: remote(
            other3.at[rows8(16 * (n // 4), 16)],
            recvs.at[rows8(32 * n0 + 16 * (1 - zh), 16)], pair(8), plane_id(zh, n),
        ).start()
    )

    wait_bytes(recv3.at[pl.ds(0, 248)], rsem.at[2])
    folded = fold_stage([recv3[pl.ds(cr, 32, stride=8), :] for cr in range(8)], fold[...], roll)
    for cr in range(8):
        send4[pl.ds(cr, 16, stride=16), :] = folded[cr][:16]
        send4[pl.ds(8 + cr, 16, stride=16), :] = folded[cr][16:]
    recv4[rows8(16 * n0, 16), :] = send4[rows8(16 * n0, 16), :]
    over_plane(
        lambda n: remote(
            send4.at[rows8(16 * n, 16)], recv4.at[rows8(16 * n0, 16)], pair(3), plane_id(zh, n)
        ).start()
    )

    wait_bytes(recvs.at[pl.ds(0, 240)], rsem.at[7])
    wait_bytes(recvs.at[pl.ds(0, 240)], rsem.at[8])
    columns = [
        jnp.concatenate([recvs[pl.ds(8 * e + 4 * c + r, 32, stride=16), :] for r in range(4)], 0)
        for c in range(2)
        for e in range(2)
    ]
    g = _dot(table_side_last, jnp.concatenate(columns, 1))
    low = _iota((16, 128), 1) < 64
    for c in range(2):
        halves = [
            g[:16, 128 * q : 128 * q + 128] - roll(g[16:, 128 * q : 128 * q + 128], 64)
            for q in (2 * c, 2 * c + 1)
        ]
        side[c] = jnp.where(low, halves[0], roll(halves[1], 64))

    wait_bytes(recv4.at[pl.ds(0, 240)], rsem.at[3])
    for a in range(2):
        rows = [
            jnp.concatenate(
                [recv4[pl.ds(8 * a + 4 * c + r, 16, stride=16), :] for r in range(4)], 0
            )
            for c in range(2)
        ]
        send5[pl.ds(a, 16, stride=2), :] = last_stage(table_last[a], rows, roll)
    recv5[rows8(8 * n0, 8), :] = send5[rows8(8 * xx, 8), :]
    over_plane(
        lambda n: remote(
            send5.at[rows8(8 * (n // 4), 8)], recv5.at[rows8(8 * n0, 8)], pair(4), plane_id(zh, n)
        ).start()
    )

    wait_bytes(recv1.at[pl.ds(0, 480)], ssem.at[0])
    wait_bytes(send2.at[pl.ds(0, 31)], ssem.at[1])
    wait_bytes(recv3.at[pl.ds(0, 248)], ssem.at[2])
    wait_bytes(recv4.at[pl.ds(0, 240)], ssem.at[3])
    wait_bytes(hop1, ssem.at[5])
    wait_bytes(hop2, ssem.at[6])
    wait_bytes(recvs.at[pl.ds(0, 240)], ssem.at[7])
    wait_bytes(recvs.at[pl.ds(0, 240)], ssem.at[8])
    for there, copy in faces:

        @pl.when(there)
        def _(copy=copy):
            copy.wait_send()

    wait_bytes(recv5.at[pl.ds(0, 120)], rsem.at[4])
    lines_y = jnp.concatenate([recv5[pl.ds(q, 16, stride=8), :] for q in range(8)], 0)
    top[...] = lines_y.T
    wait_bytes(recv5.at[pl.ds(0, 120)], ssem.at[4])


def on_device(magnetization, stiffness, residual_top, residual_side, top_kernel, side_kernel):
    tables = [jnp.asarray(t) for t in const_tables()]
    vmem = pl.BlockSpec(memory_space=pltpu.VMEM)
    anyspace = pl.BlockSpec(memory_space=pl.ANY)

    def buf(*shape):
        return pltpu.VMEM(shape, F32)

    scratch = [
        buf(4, 1152, 128), buf(2, 2, 2, 4, 2048), buf(256, 128), buf(256, 128),
        buf(32, 128), buf(512, 128), buf(32, 4, 128), buf(32, 4, 128),
        buf(128, 128), buf(256, 128), buf(256, 128), buf(256, 128), buf(32, 128), buf(128, 128),
        buf(32, 128), buf(64, 128), buf(64, 128), buf(64, 128), buf(64, 128), buf(512, 128),
        buf(64, 128), buf(64, 128), buf(64, 128), buf(64, 128),
        buf(64, 128), buf(64, 128), buf(64, 128), buf(64, 128),
        pltpu.SemaphoreType.DMA((4,)), pltpu.SemaphoreType.DMA((9,)), pltpu.SemaphoreType.DMA((9,)),
        pltpu.SemaphoreType.DMA((6,)), pltpu.SemaphoreType.DMA((6,)),
    ]
    exch, top, side = pl.pallas_call(
        body,
        out_shape=[
            jax.ShapeDtypeStruct((3, 1024, 128), F32),
            jax.ShapeDtypeStruct((128, 128), F32),
            jax.ShapeDtypeStruct((2, 16, 128), F32),
        ],
        in_specs=[anyspace, anyspace, vmem, vmem, anyspace, anyspace] + [vmem] * len(tables),
        out_specs=[vmem] * 3,
        scratch_shapes=scratch,
        compiler_params=pltpu.CompilerParams(
            collective_id=0, has_side_effects=True, vmem_limit_bytes=40 * 1024 * 1024
        ),
        name="adjoint",
    )(
        magnetization.reshape(3, 1024, 128),
        stiffness.reshape(1, 1024, 128),
        residual_top.T,
        residual_side.T,
        top_kernel,
        side_kernel,
        *tables,
    )
    exch = exch.reshape(3, 16, 64, 128)
    top = top.reshape(2, 1, 64, 128)
    side = side.reshape(2, 16, 1, 128)
    return jnp.stack([exch[0] + top[0], exch[1] + top[1] + side[0], exch[2] + side[1]])


def solution(mesh):
    placed = (
        P(None, "gz", "gx", "gy"),
        P("gz", "gx", "gy"),
        P("gx", ("gy", "gz")),
        P("gy", "gz"),
        P(None, None, ("gx", "gy", "gz"), None),
        P(None, None, ("gy", "gz"), None),
    )
    return jax.shard_map(
        on_device, mesh=mesh, in_specs=placed, out_specs=P(None, "gz", "gx", "gy"), check_vma=False
    )
```

profile of v0, /device:TPU:1, one launch (start us, length us, event | category | flops | bytes accessed | tf_op | source)
XLA Modules:
  0.0 68.1 jit_solution(11202394848860700675)
XLA Ops:
  0.0 0.0 copy-start
  0.0 1.4 %copy-done = f32[3,16,64,128]{3,2,1,0:T(8,128)S(1)} copy-done((f32[3,16,64,128]{3,2,1,0:T(8,128)S(1)}, f32[3,16,64,128]{3,2,1,0:T(8,128)}, u32[]{:S(2)}) %copy-start) | copy-done | bytes 1572888
  1.4 0.0 copy-start.1
  1.4 1.0 %copy-done.1 = f32[16,64,128]{2,1,0:T(8,128)S(1)} copy-done((f32[16,64,128]{2,1,0:T(8,128)S(1)}, f32[16,64,128]{2,1,0:T(8,128)}, u32[]{:S(2)}) %copy-start.1) | copy-done | bytes 524312
  2.5 0.0 copy-start.2
  2.5 0.9 %copy-done.2 = f32[2,2,4,2048]{3,2,1,0:T(4,128)S(1)} copy-done((f32[2,2,4,2048]{3,2,1,0:T(4,128)S(1)}, f32[2,2,4,2048]{3,2,1,0:T(4,128)}, u32[]{:S(2)}) %copy-start.2) | copy-done | bytes 131096
  3.4 0.0 copy-start.3
  3.4 0.9 %copy-done.3 = f32[2,2,4,2048]{3,2,1,0:T(4,128)S(1)} copy-done((f32[2,2,4,2048]{3,2,1,0:T(4,128)S(1)}, f32[2,2,4,2048]{3,2,1,0:T(4,128)}, u32[]{:S(2)}) %copy-start.3) | copy-done | bytes 131096
  4.3 0.0 copy-start.4
  4.3 0.8 %copy-done.4 = f32[128,32]{1,0:T(8,128)S(1)} copy-done((f32[128,32]{1,0:T(8,128)S(1)}, f32[128,32]{1,0:T(8,128)}, u32[]{:S(2)}) %copy-start.4) | copy-done | bytes 16408
  5.1 0.0 copy-start.5
  5.1 0.8 %copy-done.5 = f32[128,128]{1,0:T(8,128)S(1)} copy-done((f32[128,128]{1,0:T(8,128)S(1)}, f32[128,128]{1,0:T(8,128)}, u32[]{:S(2)}) %copy-start.5) | copy-done | bytes 65560
  5.9 0.0 copy-start.6
  5.9 0.8 %copy-done.6 = f32[64,32]{1,0:T(8,128)S(1)} copy-done((f32[64,32]{1,0:T(8,128)S(1)}, f32[64,32]{1,0:T(8,128)}, u32[]{:S(2)}) %copy-start.6) | copy-done | bytes 8216
  6.7 0.0 copy-start.7
  6.7 0.8 %copy-done.7 = f32[32,256]{1,0:T(8,128)S(1)} copy-done((f32[32,256]{1,0:T(8,128)S(1)}, f32[32,256]{1,0:T(8,128)}, u32[]{:S(2)}) %copy-start.7) | copy-done | bytes 32792
  7.5 0.0 copy-start.8
  7.5 0.7 %copy-done.8 = f32[64,32]{0,1:T(8,128)S(1)} copy-done((f32[64,32]{0,1:T(8,128)S(1)}, f32[64,32]{0,1:T(8,128)}, u32[]{:S(2)}) %copy-start.8) | copy-done | bytes 8216
  8.2 0.0 copy-start.9
  8.2 0.7 %copy-done.9 = f32[32,128]{1,0:T(8,128)S(1)} copy-done((f32[32,128]{1,0:T(8,128)S(1)}, f32[32,128]{1,0:T(8,128)}, u32[]{:S(2)}) %copy-start.9) | copy-done | bytes 16408
  8.9 0.0 copy-start.10
  8.9 0.7 %copy-done.10 = f32[32,128]{1,0:T(8,128)S(1)} copy-done((f32[32,128]{1,0:T(8,128)S(1)}, f32[32,128]{1,0:T(8,128)}, u32[]{:S(2)}) %copy-start.10) | copy-done | bytes 16408
  9.6 0.0 copy-start.11
  9.6 0.7 %copy-done.11 = f32[16,256]{1,0:T(8,128)S(1)} copy-done((f32[16,256]{1,0:T(8,128)S(1)}, f32[16,256]{1,0:T(8,128)}, u32[]{:S(2)}) %copy-start.11) | copy-done | bytes 16408
  10.3 0.0 copy-start.12
  10.3 0.7 %copy-done.12 = f32[128,16]{0,1:T(8,128)S(1)} copy-done((f32[128,16]{0,1:T(8,128)S(1)}, f32[128,16]{0,1:T(8,128)}, u32[]{:S(2)}) %copy-start.12) | copy-done | bytes 8216
  11.0 55.5 %adjoint.1 = (f32[3,1024,128]{2,1,0:T(8,128)S(1)}, f32[128,128]{1,0:T(8,128)S(1)}, f32[2,16,128]{2,1,0:T(8,128)S(1)}) custom-call(f32[3,1024,128]{2,1,0:T(8,128)S(1)} %bitcast.11, f32[1,1024,128]{2,1,0:T(8,128)S(1)} %bitcast.12, f32[32,64]{1,0:T(8,128)S(1)} %bitcast.13, f32[16,128]{1,0:T(8,128)S(1)} %bitcast.14, f32[2,2,4,2048]{3,2,1,0:T(4,128)S(1)} %copy-done.2, ...), custom_call_target="tpu_custom_call" | custom-call | tf_op jit(solution)/shard_map/adjoint/pallas_call | solution.py:511
  66.5 0.1 fusion
  66.7 0.2 add_add_fusion
  66.9 1.2 %pad_maximum_fusion = f32[3,16,64,128]{3,2,1,0:T(8,128)} fusion(f32[1,16,64,128]{3,2,1,0:T(8,128)S(1)} %get-tuple-element.19, f32[1,16,64,128]{3,2,1,0:T(8,128)S(1)} %get-tuple-element.18, f32[1,16,64,128]{3,2,1,0:T(8,128)S(1)} %broadcast_add_fusion.1), kind=kLoop, calls=%fused_computation | loop fusion | flops 786432 | bytes 3145728 | tf_op jit(solution)/shard_map/stack | solution.py:537
  (3 shorter events, 0.1 us)
Async XLA Ops:
  0.0 1.4 %copy-start = (f32[3,16,64,128]{3,2,1,0:T(8,128)S(1)}, f32[3,16,64,128]{3,2,1,0:T(8,128)}, u32[]{:S(2)}) copy-start(f32[3,16,64,128]{3,2,1,0:T(8,128)} %param.13) | copy-start | bytes 4718596
  1.4 1.0 %copy-start.1 = (f32[16,64,128]{2,1,0:T(8,128)S(1)}, f32[16,64,128]{2,1,0:T(8,128)}, u32[]{:S(2)}) copy-start(f32[16,64,128]{2,1,0:T(8,128)} %param.14) | copy-start | bytes 1572868
  2.5 0.9 %copy-start.2 = (f32[2,2,4,2048]{3,2,1,0:T(4,128)S(1)}, f32[2,2,4,2048]{3,2,1,0:T(4,128)}, u32[]{:S(2)}) copy-start(f32[2,2,4,2048]{3,2,1,0:T(4,128)} %ktop.1) | copy-start | bytes 393220
  3.4 0.9 %copy-start.3 = (f32[2,2,4,2048]{3,2,1,0:T(4,128)S(1)}, f32[2,2,4,2048]{3,2,1,0:T(4,128)}, u32[]{:S(2)}) copy-start(f32[2,2,4,2048]{3,2,1,0:T(4,128)} %kside.1) | copy-start | bytes 393220
  4.3 0.8 %copy-start.4 = (f32[128,32]{1,0:T(8,128)S(1)}, f32[128,32]{1,0:T(8,128)}, u32[]{:S(2)}) copy-start(f32[128,32]{1,0:T(8,128)} %constant.18.clone.inv) | copy-start | bytes 49156
  5.1 0.8 %copy-start.5 = (f32[128,128]{1,0:T(8,128)S(1)}, f32[128,128]{1,0:T(8,128)}, u32[]{:S(2)}) copy-start(f32[128,128]{1,0:T(8,128)} %constant.16.clone.twist) | copy-start | bytes 196612
  5.9 0.8 %copy-start.6 = (f32[64,32]{1,0:T(8,128)S(1)}, f32[64,32]{1,0:T(8,128)}, u32[]{:S(2)}) copy-start(f32[64,32]{1,0:T(8,128)} %constant.20.clone.fold) | copy-start | bytes 24580
  6.7 0.8 %copy-start.7 = (f32[32,256]{1,0:T(8,128)S(1)}, f32[32,256]{1,0:T(8,128)}, u32[]{:S(2)}) copy-start(f32[32,256]{1,0:T(8,128)} %constant.14.clone.gl32) | copy-start | bytes 98308
  7.5 0.7 %copy-start.8 = (f32[64,32]{0,1:T(8,128)S(1)}, f32[64,32]{0,1:T(8,128)}, u32[]{:S(2)}) copy-start(f32[64,32]{0,1:T(8,128)} %param.15) | copy-start | bytes 24580
  8.2 0.7 %copy-start.9 = (f32[32,128]{1,0:T(8,128)S(1)}, f32[32,128]{1,0:T(8,128)}, u32[]{:S(2)}) copy-start(f32[32,128]{1,0:T(8,128)} %constant.19.clone.back) | copy-start | bytes 49156
  8.9 0.7 %copy-start.10 = (f32[32,128]{1,0:T(8,128)S(1)}, f32[32,128]{1,0:T(8,128)}, u32[]{:S(2)}) copy-start(f32[32,128]{1,0:T(8,128)} %constant.17.clone.fwd) | copy-start | bytes 49156
  9.6 0.7 %copy-start.11 = (f32[16,256]{1,0:T(8,128)S(1)}, f32[16,256]{1,0:T(8,128)}, u32[]{:S(2)}) copy-start(f32[16,256]{1,0:T(8,128)} %constant.15.clone.gl16) | copy-start | bytes 49156
  10.3 0.7 %copy-start.12 = (f32[128,16]{0,1:T(8,128)S(1)}, f32[128,16]{0,1:T(8,128)}, u32[]{:S(2)}) copy-start(f32[128,16]{0,1:T(8,128)} %param.16) | copy-start | bytes 24580
where the time goes:
time: 69.3 us; the launch traced here: 68.1 us
  Pallas kernels  55.5 us (80%)
  local copies, waits for them, and re-layouts  11.1 us (16%)
  other arithmetic  1.45 us (2%)
    pallas_call x1, Pallas kernels, on_device(): pl.pallas_call(body, out_shape=[jax.ShapeDtypeStruct((3, 1024, 128), F32)...  55.5 us
    unnamed x26, local copies, waits for them, and re-layouts  11 us

commit v1 on v0

--- a/solution.py
+++ b/solution.py
@@ -38,7 +38,9 @@
     back = gl16.reshape(16, 2, 128).transpose(1, 0, 2).reshape(32, 128)
     c, s = _cs(i(32)[:, None], i(32)[None, :], 32)
     fold = np.concatenate([c, s], 0)
-    return [np.asarray(t, np.float32) for t in (gl32, gl16, twist, fwd, inv, back, fold)]
+    blocks = (gl32[:, :128], gl32[:, 128:], twist, fwd, inv, back, fold)
+    rows = [np.pad(t, ((0, 0), (0, 128 - t.shape[1]))) for t in blocks]
+    return np.concatenate(rows, 0).astype(np.float32)
 
 
 def _iota(shape, dim):
@@ -172,10 +174,10 @@
 
 
 def body(
-    mag, stiff, rtop, rside, ktop, kside, gl32, gl16, twist, fwd, inv, back, fold,
-    exch, top, side,
-    field, kraw, kt, ks,
-    send1, recv1, send2, recv2, send3, recv3, send4, recv4, send5, recv5,
+    mag, stiff, rtop_in, rside_in, ktop, kside, tables,
+    exch, top,
+    field, rtop, rside, tabs, kraw, kt, ks,
+    send1, recv1, recv1s, send2, recv2, send3, recv3, send4, recv4, send5, recv5,
     hop1, line1, own3, hop2, other3, recvs,
     hx_out_hi, hx_out_lo, hx_lo, hx_hi, hy_out_hi, hy_out_lo, hy_lo, hy_hi,
     local, ssem, rsem, hsend, hrecv,
@@ -221,13 +223,18 @@
     def pair(i):
         return ssem.at[i], rsem.at[i]
 
+    residuals = [
+        pltpu.make_async_copy(rtop_in, rtop, local.at[4]),
+        pltpu.make_async_copy(rside_in, rside, local.at[5]),
+    ]
     loads = [
+        pltpu.make_async_copy(tables, tabs, local.at[6]),
         pltpu.make_async_copy(mag, field.at[0:3, pl.ds(64, 1024)], local.at[0]),
         pltpu.make_async_copy(stiff, field.at[3:4, pl.ds(64, 1024)], local.at[1]),
         pltpu.make_async_copy(ktop, kraw.at[0], local.at[2]),
         pltpu.make_async_copy(kside, kraw.at[1], local.at[3]),
     ]
-    for load in loads:
+    for load in residuals + loads:
         load.start()
     barrier = pltpu.get_barrier_semaphore()
     over_plane(
@@ -241,16 +248,21 @@
     def _():
         pl.semaphore_signal(barrier, inc=1, device_id={"gy": 7 - gy}, device_id_type=MESH)
 
-    send1[0:16, :] = jnp.concatenate([rtop[0:16, :], rtop[16:32, :]], 1)
-    send1[16:32, :] = rside[...]
-    recv1[rows8(32 * n0, 32), :] = send1[...]
+    for load in residuals:
+        load.wait()
+    send1[...] = jnp.concatenate([rtop[0:16, :], rtop[16:32, :]], 1)
+    recv1[rows8(16 * n0, 16), :] = send1[...]
+    recv1s[rows8(16 * n0, 16), :] = rside[...]
     table1 = first_table(zh, n0)
     table_side = side_table(zh, n0)
 
     pl.semaphore_wait(barrier, 46 + crosses.astype(jnp.int32))
 
     over_plane(
-        lambda n: remote(send1, recv1.at[rows8(32 * n0, 32)], pair(0), plane_id(zh, n)).start()
+        lambda n: remote(send1, recv1.at[rows8(16 * n0, 16)], pair(0), plane_id(zh, n)).start()
+    )
+    over_plane(
+        lambda n: remote(rside, recv1s.at[rows8(16 * n0, 16)], pair(9), plane_id(zh, n)).start()
     )
 
     for load in loads:
@@ -315,23 +327,15 @@
                     which, cp // 2, cp % 2, :, 128 * j : 128 * j + 128
                 ]
 
-    wait_bytes(recv1.at[pl.ds(0, 480)], rsem.at[0])
-    packed = jnp.concatenate([recv1[32 * n : 32 * n + 16, :] for n in range(16)], 0)
-    first = first_stage(table1, packed, roll)
+    wait_bytes(recv1.at[pl.ds(0, 240)], rsem.at[0])
+    first = first_stage(table1, recv1[...], roll)
     for m in range(32):
         send2[m] = first[4 * m : 4 * m + 4]
     recv2[m0] = send2[m0]
     over_column(lambda m, target: remote(send2.at[m], recv2.at[m0], pair(1), target).start())
 
-    data = jnp.concatenate(
-        [
-            jnp.concatenate(
-                [recv1[32 * (4 * x + y) + 16 : 32 * (4 * x + y) + 32, :] for y in range(4)], 0
-            )
-            for x in range(4)
-        ],
-        1,
-    )
+    wait_bytes(recv1s.at[pl.ds(0, 240)], rsem.at[9])
+    data = jnp.concatenate([recv1s[64 * x : 64 * x + 64, :] for x in range(4)], 1)
     own, other = side_first(table_side, data, roll)
     for x in range(4):
         line1[rows8(32 * zh + 8 * x, 8), :] = own[x]
@@ -342,11 +346,11 @@
     table_side_last = side_last_table(gz)
 
     wait_bytes(recv2.at[pl.ds(0, 31)], rsem.at[1])
-    shared = (twist[...], fwd[...], inv[...], back[...])
+    shared = (tabs[64:192, :], tabs[192:224, :], tabs[224:352, :32], tabs[352:384, :])
     lines = line_stage(
         [recv2[:, r, :] for r in range(4)],
         lambda c, p, r: kt[64 * (2 * c + p) + 16 * r : 64 * (2 * c + p) + 16 * r + 16, :],
-        (gl32[...],) + shared,
+        (jnp.concatenate([tabs[0:32, :], tabs[32:64, :]], 1),) + shared,
         roll,
     )
     for cr in range(8):
@@ -362,7 +366,10 @@
     lines = line_stage(
         [line1[pl.ds(r, 16, stride=4), :] for r in range(4)],
         lambda c, p, r: ks[64 * (2 * c + p) + 16 * r : 64 * (2 * c + p) + 16 * r + 16, :],
-        (gl16[...],) + shared,
+        (
+            jnp.concatenate([tabs[pl.ds(0, 16, stride=2), :], tabs[pl.ds(32, 16, stride=2), :]], 1),
+        )
+        + shared,
         roll,
     )
     for cr in range(8):
@@ -427,7 +434,7 @@
     )
 
     wait_bytes(recv3.at[pl.ds(0, 248)], rsem.at[2])
-    folded = fold_stage([recv3[pl.ds(cr, 32, stride=8), :] for cr in range(8)], fold[...], roll)
+    folded = fold_stage([recv3[pl.ds(cr, 32, stride=8), :] for cr in range(8)], tabs[384:448, :32], roll)
     for cr in range(8):
         send4[pl.ds(cr, 16, stride=16), :] = folded[cr][:16]
         send4[pl.ds(8 + cr, 16, stride=16), :] = folded[cr][16:]
@@ -452,7 +459,10 @@
             g[:16, 128 * q : 128 * q + 128] - roll(g[16:, 128 * q : 128 * q + 128], 64)
             for q in (2 * c, 2 * c + 1)
         ]
-        side[c] = jnp.where(low, halves[0], roll(halves[1], 64))
+        side = jnp.where(low, halves[0], roll(halves[1], 64))
+        for z in range(16):
+            rows = slice(64 * z, 64 * z + 64)
+            exch[c + 1, rows, :] = exch[c + 1, rows, :] + side[z : z + 1, :]
 
     wait_bytes(recv4.at[pl.ds(0, 240)], rsem.at[3])
     for a in range(2):
@@ -470,7 +480,8 @@
         ).start()
     )
 
-    wait_bytes(recv1.at[pl.ds(0, 480)], ssem.at[0])
+    wait_bytes(recv1.at[pl.ds(0, 240)], ssem.at[0])
+    wait_bytes(recv1s.at[pl.ds(0, 240)], ssem.at[9])
     wait_bytes(send2.at[pl.ds(0, 31)], ssem.at[1])
     wait_bytes(recv3.at[pl.ds(0, 248)], ssem.at[2])
     wait_bytes(recv4.at[pl.ds(0, 240)], ssem.at[3])
@@ -486,55 +497,55 @@
 
     wait_bytes(recv5.at[pl.ds(0, 120)], rsem.at[4])
     lines_y = jnp.concatenate([recv5[pl.ds(q, 16, stride=8), :] for q in range(8)], 0)
-    top[...] = lines_y.T
+    top[0:128, :] = lines_y.T
+    top[128:192, :] = zero_face
     wait_bytes(recv5.at[pl.ds(0, 120)], ssem.at[4])
 
 
 def on_device(magnetization, stiffness, residual_top, residual_side, top_kernel, side_kernel):
-    tables = [jnp.asarray(t) for t in const_tables()]
+    tables = jnp.asarray(const_tables())
     vmem = pl.BlockSpec(memory_space=pltpu.VMEM)
-    anyspace = pl.BlockSpec(memory_space=pl.ANY)
+    hbm = pl.BlockSpec(memory_space=pltpu.HBM)
+
+    def pin(array):
+        return pltpu.with_memory_space_constraint(array, pltpu.HBM)
 
     def buf(*shape):
         return pltpu.VMEM(shape, F32)
 
     scratch = [
-        buf(4, 1152, 128), buf(2, 2, 2, 4, 2048), buf(256, 128), buf(256, 128),
-        buf(32, 128), buf(512, 128), buf(32, 4, 128), buf(32, 4, 128),
+        buf(4, 1152, 128), buf(32, 64), buf(16, 128), buf(448, 128), buf(2, 2, 2, 4, 2048), buf(256, 128), buf(256, 128),
+        buf(16, 128), buf(256, 128), buf(256, 128), buf(32, 4, 128), buf(32, 4, 128),
         buf(128, 128), buf(256, 128), buf(256, 128), buf(256, 128), buf(32, 128), buf(128, 128),
         buf(32, 128), buf(64, 128), buf(64, 128), buf(64, 128), buf(64, 128), buf(512, 128),
         buf(64, 128), buf(64, 128), buf(64, 128), buf(64, 128),
         buf(64, 128), buf(64, 128), buf(64, 128), buf(64, 128),
-        pltpu.SemaphoreType.DMA((4,)), pltpu.SemaphoreType.DMA((9,)), pltpu.SemaphoreType.DMA((9,)),
+        pltpu.SemaphoreType.DMA((7,)), pltpu.SemaphoreType.DMA((10,)), pltpu.SemaphoreType.DMA((10,)),
         pltpu.SemaphoreType.DMA((6,)), pltpu.SemaphoreType.DMA((6,)),
     ]
-    exch, top, side = pl.pallas_call(
+    exch, top = pl.pallas_call(
         body,
         out_shape=[
             jax.ShapeDtypeStruct((3, 1024, 128), F32),
-            jax.ShapeDtypeStruct((128, 128), F32),
-            jax.ShapeDtypeStruct((2, 16, 128), F32),
+            jax.ShapeDtypeStruct((192, 128), F32),
         ],
-        in_specs=[anyspace, anyspace, vmem, vmem, anyspace, anyspace] + [vmem] * len(tables),
-        out_specs=[vmem] * 3,
+        in_specs=[hbm] * 7,
+        out_specs=[vmem] * 2,
         scratch_shapes=scratch,
         compiler_params=pltpu.CompilerParams(
             collective_id=0, has_side_effects=True, vmem_limit_bytes=40 * 1024 * 1024
         ),
         name="adjoint",
     )(
-        magnetization.reshape(3, 1024, 128),
-        stiffness.reshape(1, 1024, 128),
-        residual_top.T,
-        residual_side.T,
-        top_kernel,
-        side_kernel,
-        *tables,
-    )
-    exch = exch.reshape(3, 16, 64, 128)
-    top = top.reshape(2, 1, 64, 128)
-    side = side.reshape(2, 16, 1, 128)
-    return jnp.stack([exch[0] + top[0], exch[1] + top[1] + side[0], exch[2] + side[1]])
+        pin(magnetization.reshape(3, 1024, 128)),
+        pin(stiffness.reshape(1, 1024, 128)),
+        pin(residual_top.T),
+        pin(residual_side.T),
+        pin(top_kernel),
+        pin(side_kernel),
+        pin(tables),
+    )
+    return exch.reshape(3, 16, 64, 128) + top.reshape(3, 1, 64, 128)
 
 
 def solution(mesh):

time: 69.3 us -> 56.7 us (0.82); the launches traced: 68.1 us -> 56.3 us
  local copies, waits for them, and re-layouts: 11.1 us -> 0 us
    unnamed x26 -> x0, local copies, waits for them, and re-layouts: 11 us -> none
    another operation x1 -> x0, other arithmetic: 1.25 us -> none  [on_device(): jnp.stack([exch[0] + top[0], exch[1] + top[1] + side[0], exch[2] + side[1]])]
    add x2 -> x1, other arithmetic: 0.2 us -> 1.35 us  [on_device(): return exch.reshape(3, 16, 64, 128) + top.reshape(3, 1, 64, 128)]
where the time goes in v1:
time: 56.7 us; the launch traced here: 56.3 us
  Pallas kernels  54.9 us (97%)
  other arithmetic  1.35 us (2%)
    pallas_call x1, Pallas kernels, on_device(): pl.pallas_call(body, out_shape=[jax.ShapeDtypeStruct((3, 1024, 128), F32)...  54.9 us
    add x1, other arithmetic, on_device(): return exch.reshape(3, 16, 64, 128) + top.reshape(3, 1, 64, 128)  1.35 us

profile of v1, /device:TPU:1, one launch (start us, length us, event | category | flops | bytes accessed | tf_op | source)
XLA Modules:
  0.0 56.3 jit_solution(11743368387981500809)
XLA Ops:
  0.0 54.9 %adjoint.1 = (f32[3,1024,128]{2,1,0:T(8,128)S(1)}, f32[192,128]{1,0:T(8,128)S(1)}) custom-call(f32[3,1024,128]{2,1,0:T(8,128)} %bitcast.8, f32[1,1024,128]{2,1,0:T(8,128)} %bitcast.9, f32[32,64]{1,0:T(8,128)} %bitcast.10, f32[16,128]{1,0:T(8,128)} %bitcast.11, f32[2,2,4,2048]{3,2,1,0:T(4,128)} %ktop.1, f32[2,2,4,2048]{3,2,1,0:T(4,128)} %kside.1, ...), custom_call_target="tpu_custom_call" | custom-call | tf_op jit(solution)/shard_map/adjoint/pallas_call | solution.py:526
  54.9 1.4 %broadcast_add_fusion = f32[3,16,64,128]{3,2,1,0:T(8,128)} fusion(f32[3,16,64,128]{3,2,1,0:T(8,128)S(1)} %bitcast.6, f32[3,64,128]{2,1,0:T(8,128)S(1)} %bitcast.7), kind=kLoop, calls=%fused_computation | loop fusion | flops 393216 | bytes 3244032 | tf_op jit(solution)/shard_map/add | solution.py:548

commit v2 on v1

--- a/solution.py
+++ b/solution.py
@@ -14,10 +14,26 @@
 SIDE_SCALE = 1.0 / (2048.0 * 128.0)
 
 
-def _dot(a, b, ca=1, cb=0):
-    return lax.dot_general(
-        a, b, (((ca,), (cb,)), ((), ())), precision=lax.Precision.HIGHEST, preferred_element_type=F32
-    )
+BF16 = jnp.bfloat16
+
+
+def _split(x):
+    high = x.astype(BF16)
+    return high, (x - high.astype(F32)).astype(BF16)
+
+
+def _left(table, axis=1):
+    high, low = _split(table)
+    return jnp.concatenate([high, high, low], axis)
+
+
+def _right(value, axis=0):
+    high, low = _split(value)
+    return jnp.concatenate([high, low, high], axis)
+
+
+def _mul(a, b, ca=1, cb=0):
+    return lax.dot_general(a, b, (((ca,), (cb,)), ((), ())), preferred_element_type=F32)
 
 
 def _cs(first, second, modulus):
@@ -38,9 +54,16 @@
     back = gl16.reshape(16, 2, 128).transpose(1, 0, 2).reshape(32, 128)
     c, s = _cs(i(32)[:, None], i(32)[None, :], 32)
     fold = np.concatenate([c, s], 0)
-    blocks = (gl32[:, :128], gl32[:, 128:], twist, fwd, inv, back, fold)
-    rows = [np.pad(t, ((0, 0), (0, 128 - t.shape[1]))) for t in blocks]
-    return np.concatenate(rows, 0).astype(np.float32)
+    turn = twist.astype(np.float32)
+    split = [split3(gl32, 0), split3(gl16, 0), split3(fwd, 1), split3(inv, 1), split3(back, 1), split3(fold, 1)]
+    return [turn] + split
+
+
+def split3(table, axis):
+    table = table.astype(np.float32)
+    high = table.astype(BF16)
+    low = (table - high.astype(np.float32)).astype(BF16)
+    return np.concatenate([high, high, low], axis)
 
 
 def _iota(shape, dim):
@@ -59,7 +82,7 @@
     parts = []
     for h in (0, 1):
         t = _angle(ky * (y + 16 * h), 2048)
-        parts += [jnp.cos(t), -jnp.sin(t)]
+        parts += [_left(jnp.cos(t)), _left(-jnp.sin(t))]
     return parts
 
 
@@ -70,7 +93,7 @@
     out = []
     for a in (0, 1):
         t = _angle(s * (32 * row + n0 + 16 * a + 512 * zh), 2048)
-        out.append(jnp.concatenate([jnp.cos(t) * TOP_SCALE, jnp.sin(t) * TOP_SCALE], 0))
+        out.append(_left(jnp.concatenate([jnp.cos(t) * TOP_SCALE, jnp.sin(t) * TOP_SCALE], 0)))
     return out
 
 
@@ -79,7 +102,7 @@
     z = _iota((16, 64), 1)
     own = jnp.where(row < 8, zh, 1 - zh)
     t = _angle((64 * own + 4 * n0 + row % 4) * z, 128)
-    return jnp.where(row % 8 < 4, jnp.cos(t), -jnp.sin(t))
+    return _left(jnp.where(row % 8 < 4, jnp.cos(t), -jnp.sin(t)))
 
 
 def side_last_table(yy):
@@ -87,17 +110,18 @@
     col = _iota((16, 128), 1)
     kz = 64 * (col % 2) + 4 * ((col // 2) % 16) + col // 32
     t = _angle(kz * (row + 16 * yy), 128)
-    return jnp.concatenate([jnp.cos(t) * SIDE_SCALE, jnp.sin(t) * SIDE_SCALE], 0)
+    return _left(jnp.concatenate([jnp.cos(t) * SIDE_SCALE, jnp.sin(t) * SIDE_SCALE], 0))
 
 
 def first_stage(w, packed, roll):
-    p = [_dot(t, packed) for t in w]
+    packed = _right(packed)
+    p = [_mul(t, packed) for t in w]
     low = _iota((128, 128), 1) < 64
     return jnp.where(low, p[0] + roll(p[2], 64), roll(p[1], 64) + p[3])
 
 
 def side_first(w, data, roll):
-    t = _dot(w, data)
+    t = _mul(w, _right(data))
     low = _iota((4, 128), 1) < 64
     own, other = [], []
     for x in range(4):
@@ -113,14 +137,14 @@
 def line_stage(rows, kernel_at, tabs, roll):
     gl, twist, fwd, inv, back = tabs
     twc, tws = twist[:64], twist[64:]
-    p = _dot(jnp.concatenate(rows, 1), gl, 0, 0)
+    p = _mul(_right(jnp.concatenate(rows, 1)), gl, 0, 0)
     mid = []
     for r in range(4):
         q = p[128 * r : 128 * r + 128]
         bre = q[:64, :128] + q[64:, 128:]
         bim = q[64:, :128] - q[:64, 128:]
         mid.append(jnp.concatenate([bre * twc + bim * tws, bim * twc - bre * tws], 0))
-    spectrum = _dot(fwd, jnp.concatenate(mid, 1))
+    spectrum = _mul(fwd, _right(jnp.concatenate(mid, 1)))
     weighted = []
     for c in range(2):
         for r in range(4):
@@ -130,13 +154,13 @@
             weighted.append(
                 jnp.concatenate([kre * sre + kim * sim, kre * sim - kim * sre], 0)
             )
-    v = _dot(inv, jnp.concatenate(weighted, 1))
+    v = _mul(inv, _right(jnp.concatenate(weighted, 1)))
     turned = []
     for cr in range(8):
         vre = v[:64, 128 * cr : 128 * cr + 128]
         vim = v[64:, 128 * cr : 128 * cr + 128]
         turned += [vre * twc - vim * tws, vim * twc + vre * tws]
-    u = _dot(back, jnp.concatenate(turned, 0), 1, 1)
+    u = _mul(back, _right(jnp.concatenate(turned, 0), 1), 1, 1)
     return spread(u, 16, roll)
 
 
@@ -150,11 +174,11 @@
 
 
 def fold_stage(rows, fold, roll):
-    return spread(_dot(fold, jnp.concatenate(rows, 1)), 32, roll)
+    return spread(_mul(fold, _right(jnp.concatenate(rows, 1))), 32, roll)
 
 
 def last_stage(table, rows, roll):
-    g = _dot(table, jnp.concatenate(rows, 1))
+    g = _mul(table, _right(jnp.concatenate(rows, 1)))
     low = _iota((16, 128), 1) < 64
     part = [g[:16, 128 * c : 128 * c + 128] - roll(g[16:, 128 * c : 128 * c + 128], 64) for c in (0, 1)]
     return jnp.where(low, part[0], roll(part[1], 64))
@@ -174,9 +198,9 @@
 
 
 def body(
-    mag, stiff, rtop_in, rside_in, ktop, kside, tables,
+    mag, stiff, rtop_in, rside_in, ktop, kside, c_turn, c_gl32, c_gl16, c_fwd, c_inv, c_back, c_fold,
     exch, top,
-    field, rtop, rside, tabs, kraw, kt, ks,
+    field, rtop, rside, twist, gl32, gl16, fwd, inv, back, fold, kraw, kt, ks,
     send1, recv1, recv1s, send2, recv2, send3, recv3, send4, recv4, send5, recv5,
     hop1, line1, own3, hop2, other3, recvs,
     hx_out_hi, hx_out_lo, hx_lo, hx_hi, hy_out_hi, hy_out_lo, hy_lo, hy_hi,
@@ -228,7 +252,11 @@
         pltpu.make_async_copy(rside_in, rside, local.at[5]),
     ]
     loads = [
-        pltpu.make_async_copy(tables, tabs, local.at[6]),
+        pltpu.make_async_copy(src, dst, local.at[6 + i])
+        for i, (src, dst) in enumerate(
+            [(c_turn, twist), (c_gl32, gl32), (c_gl16, gl16), (c_fwd, fwd), (c_inv, inv), (c_back, back), (c_fold, fold)]
+        )
+    ] + [
         pltpu.make_async_copy(mag, field.at[0:3, pl.ds(64, 1024)], local.at[0]),
         pltpu.make_async_copy(stiff, field.at[3:4, pl.ds(64, 1024)], local.at[1]),
         pltpu.make_async_copy(ktop, kraw.at[0], local.at[2]),
@@ -253,8 +281,6 @@
     send1[...] = jnp.concatenate([rtop[0:16, :], rtop[16:32, :]], 1)
     recv1[rows8(16 * n0, 16), :] = send1[...]
     recv1s[rows8(16 * n0, 16), :] = rside[...]
-    table1 = first_table(zh, n0)
-    table_side = side_table(zh, n0)
 
     pl.semaphore_wait(barrier, 46 + crosses.astype(jnp.int32))
 
@@ -327,6 +353,11 @@
                     which, cp // 2, cp % 2, :, 128 * j : 128 * j + 128
                 ]
 
+    table1 = first_table(zh, n0)
+    table_side = side_table(zh, n0)
+    table_last = last_table(zh, n0)
+    table_side_last = side_last_table(gz)
+
     wait_bytes(recv1.at[pl.ds(0, 240)], rsem.at[0])
     first = first_stage(table1, recv1[...], roll)
     for m in range(32):
@@ -342,15 +373,12 @@
         hop1[8 * x : 8 * x + 8, :] = other[x]
     remote(hop1, line1.at[rows8(32 * zh, 32)], pair(5), far).start()
 
-    table_last = last_table(zh, n0)
-    table_side_last = side_last_table(gz)
-
     wait_bytes(recv2.at[pl.ds(0, 31)], rsem.at[1])
-    shared = (tabs[64:192, :], tabs[192:224, :], tabs[224:352, :32], tabs[352:384, :])
+    shared = (twist[...], fwd[...], inv[...], back[...])
     lines = line_stage(
         [recv2[:, r, :] for r in range(4)],
         lambda c, p, r: kt[64 * (2 * c + p) + 16 * r : 64 * (2 * c + p) + 16 * r + 16, :],
-        (jnp.concatenate([tabs[0:32, :], tabs[32:64, :]], 1),) + shared,
+        (gl32[...],) + shared,
         roll,
     )
     for cr in range(8):
@@ -366,10 +394,7 @@
     lines = line_stage(
         [line1[pl.ds(r, 16, stride=4), :] for r in range(4)],
         lambda c, p, r: ks[64 * (2 * c + p) + 16 * r : 64 * (2 * c + p) + 16 * r + 16, :],
-        (
-            jnp.concatenate([tabs[pl.ds(0, 16, stride=2), :], tabs[pl.ds(32, 16, stride=2), :]], 1),
-        )
-        + shared,
+        (gl16[...],) + shared,
         roll,
     )
     for cr in range(8):
@@ -434,7 +459,7 @@
     )
 
     wait_bytes(recv3.at[pl.ds(0, 248)], rsem.at[2])
-    folded = fold_stage([recv3[pl.ds(cr, 32, stride=8), :] for cr in range(8)], tabs[384:448, :32], roll)
+    folded = fold_stage([recv3[pl.ds(cr, 32, stride=8), :] for cr in range(8)], fold[...], roll)
     for cr in range(8):
         send4[pl.ds(cr, 16, stride=16), :] = folded[cr][:16]
         send4[pl.ds(8 + cr, 16, stride=16), :] = folded[cr][16:]
@@ -452,7 +477,7 @@
         for c in range(2)
         for e in range(2)
     ]
-    g = _dot(table_side_last, jnp.concatenate(columns, 1))
+    g = _mul(table_side_last, _right(jnp.concatenate(columns, 1)))
     low = _iota((16, 128), 1) < 64
     for c in range(2):
         halves = [
@@ -503,7 +528,7 @@
 
 
 def on_device(magnetization, stiffness, residual_top, residual_side, top_kernel, side_kernel):
-    tables = jnp.asarray(const_tables())
+    tables = [jnp.asarray(t) for t in const_tables()]
     vmem = pl.BlockSpec(memory_space=pltpu.VMEM)
     hbm = pl.BlockSpec(memory_space=pltpu.HBM)
 
@@ -514,13 +539,13 @@
         return pltpu.VMEM(shape, F32)
 
     scratch = [
-        buf(4, 1152, 128), buf(32, 64), buf(16, 128), buf(448, 128), buf(2, 2, 2, 4, 2048), buf(256, 128), buf(256, 128),
+        buf(4, 1152, 128), buf(32, 64), buf(16, 128), *[pltpu.VMEM(t.shape, t.dtype) for t in tables], buf(2, 2, 2, 4, 2048), buf(256, 128), buf(256, 128),
         buf(16, 128), buf(256, 128), buf(256, 128), buf(32, 4, 128), buf(32, 4, 128),
         buf(128, 128), buf(256, 128), buf(256, 128), buf(256, 128), buf(32, 128), buf(128, 128),
         buf(32, 128), buf(64, 128), buf(64, 128), buf(64, 128), buf(64, 128), buf(512, 128),
         buf(64, 128), buf(64, 128), buf(64, 128), buf(64, 128),
         buf(64, 128), buf(64, 128), buf(64, 128), buf(64, 128),
-        pltpu.SemaphoreType.DMA((7,)), pltpu.SemaphoreType.DMA((10,)), pltpu.SemaphoreType.DMA((10,)),
+        pltpu.SemaphoreType.DMA((13,)), pltpu.SemaphoreType.DMA((10,)), pltpu.SemaphoreType.DMA((10,)),
         pltpu.SemaphoreType.DMA((6,)), pltpu.SemaphoreType.DMA((6,)),
     ]
     exch, top = pl.pallas_call(
@@ -529,7 +554,7 @@
             jax.ShapeDtypeStruct((3, 1024, 128), F32),
             jax.ShapeDtypeStruct((192, 128), F32),
         ],
-        in_specs=[hbm] * 7,
+        in_specs=[hbm] * (6 + len(tables)),
         out_specs=[vmem] * 2,
         scratch_shapes=scratch,
         compiler_params=pltpu.CompilerParams(
@@ -543,7 +568,7 @@
         pin(residual_side.T),
         pin(top_kernel),
         pin(side_kernel),
-        pin(tables),
+        *[pin(t) for t in tables],
     )
     return exch.reshape(3, 16, 64, 128) + top.reshape(3, 1, 64, 128)
 

time: 56.7 us -> 55.1 us (0.972)
  the two profiles are of different devices: /device:TPU:1 before, /device:TPU:32 now
where the time goes in v2:
time: 55.1 us; the launch traced here: 55 us
  Pallas kernels  53.6 us (97%)
  other arithmetic  1.35 us (2%)
    pallas_call x1, Pallas kernels, on_device(): pl.pallas_call(body, out_shape=[jax.ShapeDtypeStruct((3, 1024, 128), F32)...  53.6 us
    add x1, other arithmetic, on_device(): return exch.reshape(3, 16, 64, 128) + top.reshape(3, 1, 64, 128)  1.35 us

profile of v2, /device:TPU:32, one launch (start us, length us, event | category | flops | bytes accessed | tf_op | source)
XLA Modules:
  0.0 55.0 jit_solution(15014090453846727843)
XLA Ops:
  0.0 53.6 %adjoint.1 = (f32[3,1024,128]{2,1,0:T(8,128)S(1)}, f32[192,128]{1,0:T(8,128)S(1)}) custom-call(f32[3,1024,128]{2,1,0:T(8,128)} %bitcast.8, f32[1,1024,128]{2,1,0:T(8,128)} %bitcast.9, f32[32,64]{1,0:T(8,128)} %bitcast.10, f32[16,128]{1,0:T(8,128)} %bitcast.11, f32[2,2,4,2048]{3,2,1,0:T(4,128)} %ktop.1, f32[2,2,4,2048]{3,2,1,0:T(4,128)} %kside.1, ...), custom_call_target="tpu_custom_call" | custom-call | tf_op jit(solution)/shard_map/adjoint/pallas_call | solution.py:551
  53.6 1.4 %broadcast_add_fusion = f32[3,16,64,128]{3,2,1,0:T(8,128)} fusion(f32[3,16,64,128]{3,2,1,0:T(8,128)S(1)} %bitcast.6, f32[3,64,128]{2,1,0:T(8,128)S(1)} %bitcast.7), kind=kLoop, calls=%fused_computation | loop fusion | flops 393216 | bytes 3244032 | tf_op jit(solution)/shard_map/add | solution.py:573

commit v3 on v2

--- a/solution.py
+++ b/solution.py
@@ -204,14 +204,14 @@
     send1, recv1, recv1s, send2, recv2, send3, recv3, send4, recv4, send5, recv5,
     hop1, line1, own3, hop2, other3, recvs,
     hx_out_hi, hx_out_lo, hx_lo, hx_hi, hy_out_hi, hy_out_lo, hy_lo, hy_hi,
-    local, ssem, rsem, hsend, hrecv,
+    local, ssem, rsem, hsend, hrecv, near, cross,
 ):
     gx, gy, gz = lax.axis_index("gx"), lax.axis_index("gy"), lax.axis_index("gz")
     zh, xx = gy // 4, gy % 4
     n0 = 4 * xx + gz
     m0 = 2 * gx + zh
     v0 = 2 * (8 * zh + gx // 2) + gx % 2
-    crosses = jnp.logical_or(gy == 3, gy == 4)
+    z, core = 8 * zh + gx // 2, gx % 2
     far = {"gx": (gx + 8) % 16, "gy": 4 * (1 - zh) + xx}
 
     def roll(value, shift):
@@ -233,6 +233,13 @@
             return carry
 
         lax.fori_loop(0, 31, step, 0)
+
+    def in_column(at, which):
+        at = (at + 16) % 16
+        return {"gx": 2 * (at % 8) + which, "gy": 4 * (at // 8) + xx}
+
+    def signal(sem, target):
+        pl.semaphore_signal(sem, inc=1, device_id=target, device_id_type=MESH)
 
     def remote(src, dst, sems, target):
         send_sem, recv_sem = sems
@@ -265,16 +272,14 @@
     for load in residuals + loads:
         load.start()
     barrier = pltpu.get_barrier_semaphore()
-    over_plane(
-        lambda n: pl.semaphore_signal(barrier, inc=1, device_id=plane_id(zh, n), device_id_type=MESH)
-    )
-    over_column(
-        lambda m, target: pl.semaphore_signal(barrier, inc=1, device_id=target, device_id_type=MESH)
-    )
-
-    @pl.when(crosses)
-    def _():
-        pl.semaphore_signal(barrier, inc=1, device_id={"gy": 7 - gy}, device_id_type=MESH)
+    over_plane(lambda n: signal(barrier, plane_id(zh, n)))
+
+    def greet(k, carry):
+        k = jnp.where(k < 8, k, k + 1)
+        signal(barrier, in_column(z + k // 2 - 4, (core + k % 2) % 2))
+        return carry
+
+    lax.fori_loop(0, 17, greet, 0)
 
     for load in residuals:
         load.wait()
@@ -282,7 +287,7 @@
     recv1[rows8(16 * n0, 16), :] = send1[...]
     recv1s[rows8(16 * n0, 16), :] = rside[...]
 
-    pl.semaphore_wait(barrier, 46 + crosses.astype(jnp.int32))
+    pl.semaphore_wait(barrier, 32)
 
     over_plane(
         lambda n: remote(send1, recv1.at[rows8(16 * n0, 16)], pair(0), plane_id(zh, n)).start()
@@ -290,6 +295,9 @@
     over_plane(
         lambda n: remote(rside, recv1s.at[rows8(16 * n0, 16)], pair(9), plane_id(zh, n)).start()
     )
+
+    signal(near, in_column(z + 4, core))
+    signal(near, in_column(z - 4, core))
 
     for load in loads:
         load.wait()
@@ -327,7 +335,11 @@
                (hsend.at[5], hrecv.at[5]), {"gz": (gz + 3) % 4}),
     )
     faces = (y_up, y_dn, z_up, z_dn, x_up, x_dn)
-    for there, copy in faces:
+    inside = (
+        (jnp.logical_and(gy < 7, gy != 3), y_up[1]),
+        (jnp.logical_and(gy > 0, gy != 4), y_dn[1]),
+    ) + faces[2:]
+    for there, copy in inside:
 
         @pl.when(there)
         def _(copy=copy):
@@ -358,12 +370,27 @@
     table_last = last_table(zh, n0)
     table_side_last = side_last_table(gz)
 
+    pl.semaphore_wait(near, 2)
+
+    for at in (0, 7):
+
+        @pl.when(gy == at)
+        def _(at=at):
+            signal(cross, {"gy": 3 if at == 0 else 4})
+
     wait_bytes(recv1.at[pl.ds(0, 240)], rsem.at[0])
     first = first_stage(table1, recv1[...], roll)
     for m in range(32):
         send2[m] = first[4 * m : 4 * m + 4]
     recv2[m0] = send2[m0]
     over_column(lambda m, target: remote(send2.at[m], recv2.at[m0], pair(1), target).start())
+
+    for at, copy in ((3, y_up[1]), (4, y_dn[1])):
+
+        @pl.when(gy == at)
+        def _(copy=copy):
+            pl.semaphore_wait(cross, 1)
+            copy.start()
 
     wait_bytes(recv1s.at[pl.ds(0, 240)], rsem.at[9])
     data = jnp.concatenate([recv1s[64 * x : 64 * x + 64, :] for x in range(4)], 1)
@@ -547,6 +574,7 @@
         buf(64, 128), buf(64, 128), buf(64, 128), buf(64, 128),
         pltpu.SemaphoreType.DMA((13,)), pltpu.SemaphoreType.DMA((10,)), pltpu.SemaphoreType.DMA((10,)),
         pltpu.SemaphoreType.DMA((6,)), pltpu.SemaphoreType.DMA((6,)),
+        pltpu.SemaphoreType.REGULAR, pltpu.SemaphoreType.REGULAR,
     ]
     exch, top = pl.pallas_call(
         body,

time: 55.1 us -> 53 us (0.962)
  the two profiles are of different devices: /device:TPU:32 before, /device:TPU:96 now
where the time goes in v3:
time: 53 us; the launch traced here: 52.9 us
  Pallas kernels  51.5 us (97%)
  other arithmetic  1.35 us (3%)
    pallas_call x1, Pallas kernels, on_device(): pl.pallas_call(body, out_shape=[jax.ShapeDtypeStruct((3, 1024, 128), F32)...  51.5 us
    add x1, other arithmetic, on_device(): return exch.reshape(3, 16, 64, 128) + top.reshape(3, 1, 64, 128)  1.35 us

profile of v3, /device:TPU:96, one launch (start us, length us, event | category | flops | bytes accessed | tf_op | source)
XLA Modules:
  0.0 52.9 jit_solution(6824414343055666197)
XLA Ops:
  0.0 51.5 %adjoint.1 = (f32[3,1024,128]{2,1,0:T(8,128)S(1)}, f32[192,128]{1,0:T(8,128)S(1)}) custom-call(f32[3,1024,128]{2,1,0:T(8,128)} %bitcast.8, f32[1,1024,128]{2,1,0:T(8,128)} %bitcast.9, f32[32,64]{1,0:T(8,128)} %bitcast.10, f32[16,128]{1,0:T(8,128)} %bitcast.11, f32[2,2,4,2048]{3,2,1,0:T(4,128)} %ktop.1, f32[2,2,4,2048]{3,2,1,0:T(4,128)} %kside.1, ...), custom_call_target="tpu_custom_call" | custom-call | tf_op jit(solution)/shard_map/adjoint/pallas_call | solution.py:579
  51.5 1.4 %broadcast_add_fusion = f32[3,16,64,128]{3,2,1,0:T(8,128)} fusion(f32[3,16,64,128]{3,2,1,0:T(8,128)S(1)} %bitcast.6, f32[3,64,128]{2,1,0:T(8,128)S(1)} %bitcast.7), kind=kLoop, calls=%fused_computation | loop fusion | flops 393216 | bytes 3244032 | tf_op jit(solution)/shard_map/add | solution.py:601

commit v4 on v3

--- a/solution.py
+++ b/solution.py
@@ -9,7 +9,11 @@
 from jax.sharding import PartitionSpec as P
 
 F32 = jnp.float32
-MESH = pl.DeviceIdType.MESH
+LOGICAL = pl.DeviceIdType.LOGICAL
+PLANE_ORDER = sorted(
+    [(dx, dy) for dx in range(4) for dy in range(4) if dx or dy],
+    key=lambda d: -(min(d[0], 4 - d[0]) + min(d[1], 4 - d[1])),
+)
 TOP_SCALE = 1.0 / 2048.0**2
 SIDE_SCALE = 1.0 / (2048.0 * 128.0)
 
@@ -184,15 +188,6 @@
     return jnp.where(low, part[0], roll(part[1], 64))
 
 
-def plane_id(zh, n):
-    return {"gy": 4 * zh + n // 4, "gz": n % 4}
-
-
-def ring_place(v):
-    z = v // 2
-    return 2 * (z % 8) + v % 2, z // 8
-
-
 def rows8(start, size):
     return pl.ds(pl.multiple_of(start, 8), size)
 
@@ -207,45 +202,53 @@
     local, ssem, rsem, hsend, hrecv, near, cross,
 ):
     gx, gy, gz = lax.axis_index("gx"), lax.axis_index("gy"), lax.axis_index("gz")
-    zh, xx = gy // 4, gy % 4
+    zh, xx = lax.div(gy, 4), lax.rem(gy, 4)
     n0 = 4 * xx + gz
     m0 = 2 * gx + zh
-    v0 = 2 * (8 * zh + gx // 2) + gx % 2
-    z, core = 8 * zh + gx // 2, gx % 2
-    far = {"gx": (gx + 8) % 16, "gy": 4 * (1 - zh) + xx}
+    z, core = 8 * zh + lax.div(gx, 2), lax.rem(gx, 2)
+    device = 16 * m0 + n0
+
+    def column_index(z_plus, which):
+        at = lax.rem(z_plus, 16)
+        return 4 * lax.rem(at, 8) + 2 * which + lax.div(at, 8)
+
+    def plane_id(n):
+        return 16 * m0 + n
+
+    def column_id(m):
+        return 16 * m + n0
+
+    far = jnp.where(lax.rem(gx, 16) < 8, column_id(2 * (gx + 8) + 1 - zh), column_id(2 * (gx - 8) + 1 - zh))
 
     def roll(value, shift):
         return pltpu.roll(value, shift, 1)
 
     def over_plane(action):
+        for dx, dy in PLANE_ORDER:
+            x = lax.rem(xx + dx, 4)
+            action(4 * x + lax.rem(gz + dy, 4), x)
+
+    def over_column(action):
+        for which in (0, 1):
+            action(column_index(z + 8, which))
+
         def step(k, carry):
-            action((n0 + k) % 16)
+            for which in (0, 1):
+                action(column_index(z + 8 - k, which))
+                action(column_index(z + 8 + k, which))
             return carry
 
-        lax.fori_loop(1, 16, step, 0)
-
-    def over_column(action):
-        def step(k, carry):
-            half = (k + 1) // 2
-            off = jnp.where(k % 2 == 1, 16 - half, 16 + half)
-            px, ph = ring_place((v0 + off) % 32)
-            action(2 * px + ph, {"gx": px, "gy": 4 * ph + xx})
-            return carry
-
-        lax.fori_loop(0, 31, step, 0)
-
-    def in_column(at, which):
-        at = (at + 16) % 16
-        return {"gx": 2 * (at % 8) + which, "gy": 4 * (at // 8) + xx}
+        lax.fori_loop(1, 8, step, 0)
+        action(column_index(z, 1 - core))
 
     def signal(sem, target):
-        pl.semaphore_signal(sem, inc=1, device_id=target, device_id_type=MESH)
+        pl.semaphore_signal(sem, inc=1, device_id=target, device_id_type=LOGICAL)
 
     def remote(src, dst, sems, target):
         send_sem, recv_sem = sems
         return pltpu.make_async_remote_copy(
             src_ref=src, dst_ref=dst, send_sem=send_sem, recv_sem=recv_sem,
-            device_id=target, device_id_type=MESH,
+            device_id=target, device_id_type=LOGICAL,
         )
 
     def wait_bytes(ref, sem):
@@ -272,14 +275,16 @@
     for load in residuals + loads:
         load.start()
     barrier = pltpu.get_barrier_semaphore()
-    over_plane(lambda n: signal(barrier, plane_id(zh, n)))
+    over_plane(lambda n, x: signal(barrier, plane_id(n)))
 
     def greet(k, carry):
-        k = jnp.where(k < 8, k, k + 1)
-        signal(barrier, in_column(z + k // 2 - 4, (core + k % 2) % 2))
+        for which in (0, 1):
+            signal(barrier, column_id(column_index(z + k, which)))
+            signal(barrier, column_id(column_index(z + 16 - k, which)))
         return carry
 
-    lax.fori_loop(0, 17, greet, 0)
+    lax.fori_loop(1, 5, greet, 0)
+    signal(barrier, column_id(column_index(z, 1 - core)))
 
     for load in residuals:
         load.wait()
@@ -290,14 +295,14 @@
     pl.semaphore_wait(barrier, 32)
 
     over_plane(
-        lambda n: remote(send1, recv1.at[rows8(16 * n0, 16)], pair(0), plane_id(zh, n)).start()
+        lambda n, x: remote(send1, recv1.at[rows8(16 * n0, 16)], pair(0), plane_id(n)).start()
     )
     over_plane(
-        lambda n: remote(rside, recv1s.at[rows8(16 * n0, 16)], pair(9), plane_id(zh, n)).start()
-    )
-
-    signal(near, in_column(z + 4, core))
-    signal(near, in_column(z - 4, core))
+        lambda n, x: remote(rside, recv1s.at[rows8(16 * n0, 16)], pair(9), plane_id(n)).start()
+    )
+
+    signal(near, column_id(column_index(z + 4, core)))
+    signal(near, column_id(column_index(z + 12, core)))
 
     for load in loads:
         load.wait()
@@ -320,26 +325,22 @@
     hy_out_hi[...] = packed_hi
     hy_out_lo[...] = packed_lo
 
-    x_up = (gx < 15, remote(hx_out_hi, hx_lo, (hsend.at[0], hrecv.at[0]), {"gx": (gx + 1) % 16}))
-    x_dn = (gx > 0, remote(hx_out_lo, hx_hi, (hsend.at[1], hrecv.at[1]), {"gx": (gx + 15) % 16}))
-    y_up = (gy < 7, remote(hy_out_hi, hy_lo, (hsend.at[2], hrecv.at[2]), {"gy": (gy + 1) % 8}))
-    y_dn = (gy > 0, remote(hy_out_lo, hy_hi, (hsend.at[3], hrecv.at[3]), {"gy": (gy + 7) % 8}))
+    x_up = (gx < 15, remote(hx_out_hi, hx_lo, (hsend.at[0], hrecv.at[0]), device + 32))
+    x_dn = (gx > 0, remote(hx_out_lo, hx_hi, (hsend.at[1], hrecv.at[1]), device - 32))
+    y_up = (gy < 7, remote(hy_out_hi, hy_lo, (hsend.at[2], hrecv.at[2]), device + 4))
+    y_dn = (gy > 0, remote(hy_out_lo, hy_hi, (hsend.at[3], hrecv.at[3]), device - 4))
     z_up = (
         gz < 3,
         remote(field.at[:, pl.ds(1024, 64)], field.at[:, pl.ds(0, 64)],
-               (hsend.at[4], hrecv.at[4]), {"gz": (gz + 1) % 4}),
+               (hsend.at[4], hrecv.at[4]), device + 1),
     )
     z_dn = (
         gz > 0,
         remote(field.at[:, pl.ds(64, 64)], field.at[:, pl.ds(1088, 64)],
-               (hsend.at[5], hrecv.at[5]), {"gz": (gz + 3) % 4}),
+               (hsend.at[5], hrecv.at[5]), device - 1),
     )
     faces = (y_up, y_dn, z_up, z_dn, x_up, x_dn)
-    inside = (
-        (jnp.logical_and(gy < 7, gy != 3), y_up[1]),
-        (jnp.logical_and(gy > 0, gy != 4), y_dn[1]),
-    ) + faces[2:]
-    for there, copy in inside:
+    for there, copy in faces[4:]:
 
         @pl.when(there)
         def _(copy=copy):
@@ -376,20 +377,23 @@
 
         @pl.when(gy == at)
         def _(at=at):
-            signal(cross, {"gy": 3 if at == 0 else 4})
+            signal(cross, device + (12 if at == 0 else -12))
 
     wait_bytes(recv1.at[pl.ds(0, 240)], rsem.at[0])
     first = first_stage(table1, recv1[...], roll)
     for m in range(32):
         send2[m] = first[4 * m : 4 * m + 4]
     recv2[m0] = send2[m0]
-    over_column(lambda m, target: remote(send2.at[m], recv2.at[m0], pair(1), target).start())
-
-    for at, copy in ((3, y_up[1]), (4, y_dn[1])):
-
-        @pl.when(gy == at)
+    over_column(lambda m: remote(send2.at[m], recv2.at[m0], pair(1), column_id(m)).start())
+
+    @pl.when(jnp.logical_or(gy == 3, gy == 4))
+    def _():
+        pl.semaphore_wait(cross, 1)
+
+    for there, copy in faces[:4]:
+
+        @pl.when(there)
         def _(copy=copy):
-            pl.semaphore_wait(cross, 1)
             copy.start()
 
     wait_bytes(recv1s.at[pl.ds(0, 240)], rsem.at[9])
@@ -412,8 +416,8 @@
         send3[pl.ds(cr, 16, stride=8), :] = lines[cr]
     recv3[rows8(8 * m0, 8), :] = send3[rows8(8 * gx, 8), :]
     over_column(
-        lambda m, target: remote(
-            send3.at[rows8(8 * (m // 2), 8)], recv3.at[rows8(8 * m0, 8)], pair(2), target
+        lambda m: remote(
+            send3.at[rows8(8 * lax.div(m, 2), 8)], recv3.at[rows8(8 * m0, 8)], pair(2), column_id(m)
         ).start()
     )
 
@@ -431,9 +435,9 @@
     remote(hop2, other3, pair(6), far).start()
     recvs[rows8(32 * n0 + 16 * zh, 16), :] = own3[rows8(16 * xx, 16), :]
     over_plane(
-        lambda n: remote(
-            own3.at[rows8(16 * (n // 4), 16)],
-            recvs.at[rows8(32 * n0 + 16 * zh, 16)], pair(7), plane_id(zh, n),
+        lambda n, x: remote(
+            own3.at[rows8(16 * x, 16)],
+            recvs.at[rows8(32 * n0 + 16 * zh, 16)], pair(7), plane_id(n),
         ).start()
     )
 
@@ -479,9 +483,9 @@
     wait_bytes(other3, rsem.at[6])
     recvs[rows8(32 * n0 + 16 * (1 - zh), 16), :] = other3[rows8(16 * xx, 16), :]
     over_plane(
-        lambda n: remote(
-            other3.at[rows8(16 * (n // 4), 16)],
-            recvs.at[rows8(32 * n0 + 16 * (1 - zh), 16)], pair(8), plane_id(zh, n),
+        lambda n, x: remote(
+            other3.at[rows8(16 * x, 16)],
+            recvs.at[rows8(32 * n0 + 16 * (1 - zh), 16)], pair(8), plane_id(n),
         ).start()
     )
 
@@ -492,8 +496,8 @@
         send4[pl.ds(8 + cr, 16, stride=16), :] = folded[cr][16:]
     recv4[rows8(16 * n0, 16), :] = send4[rows8(16 * n0, 16), :]
     over_plane(
-        lambda n: remote(
-            send4.at[rows8(16 * n, 16)], recv4.at[rows8(16 * n0, 16)], pair(3), plane_id(zh, n)
+        lambda n, x: remote(
+            send4.at[rows8(16 * n, 16)], recv4.at[rows8(16 * n0, 16)], pair(3), plane_id(n)
         ).start()
     )
 
@@ -527,8 +531,8 @@
         send5[pl.ds(a, 16, stride=2), :] = last_stage(table_last[a], rows, roll)
     recv5[rows8(8 * n0, 8), :] = send5[rows8(8 * xx, 8), :]
     over_plane(
-        lambda n: remote(
-            send5.at[rows8(8 * (n // 4), 8)], recv5.at[rows8(8 * n0, 8)], pair(4), plane_id(zh, n)
+        lambda n, x: remote(
+            send5.at[rows8(8 * x, 8)], recv5.at[rows8(8 * n0, 8)], pair(4), plane_id(n)
         ).start()
     )
 

time: 53 us -> 52.5 us (level)
  the two profiles are of different devices: /device:TPU:96 before, /device:TPU:32 now
where the time goes in v4:
time: 52.5 us; the launch traced here: 52.3 us
  Pallas kernels  51 us (97%)
  other arithmetic  1.35 us (3%)
    pallas_call x1, Pallas kernels, on_device(): pl.pallas_call(body, out_shape=[jax.ShapeDtypeStruct((3, 1024, 128), F32)...  51 us
    add x1, other arithmetic, on_device(): return exch.reshape(3, 16, 64, 128) + top.reshape(3, 1, 64, 128)  1.35 us

profile of v4, /device:TPU:32, one launch (start us, length us, event | category | flops | bytes accessed | tf_op | source)
XLA Modules:
  0.0 52.3 jit_solution(710499820641562912)
XLA Ops:
  0.0 51.0 %adjoint.1 = (f32[3,1024,128]{2,1,0:T(8,128)S(1)}, f32[192,128]{1,0:T(8,128)S(1)}) custom-call(f32[3,1024,128]{2,1,0:T(8,128)} %bitcast.8, f32[1,1024,128]{2,1,0:T(8,128)} %bitcast.9, f32[32,64]{1,0:T(8,128)} %bitcast.10, f32[16,128]{1,0:T(8,128)} %bitcast.11, f32[2,2,4,2048]{3,2,1,0:T(4,128)} %ktop.1, f32[2,2,4,2048]{3,2,1,0:T(4,128)} %kside.1, ...), custom_call_target="tpu_custom_call" | custom-call | tf_op jit(solution)/shard_map/adjoint/pallas_call | solution.py:583
  51.0 1.4 %broadcast_add_fusion = f32[3,16,64,128]{3,2,1,0:T(8,128)} fusion(f32[3,16,64,128]{3,2,1,0:T(8,128)S(1)} %bitcast.6, f32[3,64,128]{2,1,0:T(8,128)S(1)} %bitcast.7), kind=kLoop, calls=%fused_computation | loop fusion | flops 393216 | bytes 3244032 | tf_op jit(solution)/shard_map/add | solution.py:605

commit v5 on v4

--- a/solution.py
+++ b/solution.py
@@ -109,10 +109,10 @@
     return _left(jnp.where(row % 8 < 4, jnp.cos(t), -jnp.sin(t)))
 
 
-def side_last_table(yy):
-    row = _iota((16, 128), 0)
-    col = _iota((16, 128), 1)
-    kz = 64 * (col % 2) + 4 * ((col // 2) % 16) + col // 32
+def side_last_table(zh, yy):
+    row = _iota((16, 64), 0)
+    col = _iota((16, 64), 1)
+    kz = 64 * zh + 4 * (col % 16) + col // 16
     t = _angle(kz * (row + 16 * yy), 128)
     return _left(jnp.concatenate([jnp.cos(t) * SIDE_SCALE, jnp.sin(t) * SIDE_SCALE], 0))
 
@@ -197,8 +197,8 @@
     exch, top,
     field, rtop, rside, twist, gl32, gl16, fwd, inv, back, fold, kraw, kt, ks,
     send1, recv1, recv1s, send2, recv2, send3, recv3, send4, recv4, send5, recv5,
-    hop1, line1, own3, hop2, other3, recvs,
-    hx_out_hi, hx_out_lo, hx_lo, hx_hi, hy_out_hi, hy_out_lo, hy_lo, hy_hi,
+    hop1, line1, send6, recv6, hop2, other2,
+    hx_out_hi, hx_out_lo, hx_lo, hx_hi, hy_out_hi, hy_out_lo, hy_lo, hy_hi, col_lo, col_hi,
     local, ssem, rsem, hsend, hrecv, near, cross,
 ):
     gx, gy, gz = lax.axis_index("gx"), lax.axis_index("gy"), lax.axis_index("gz")
@@ -298,7 +298,7 @@
         lambda n, x: remote(send1, recv1.at[rows8(16 * n0, 16)], pair(0), plane_id(n)).start()
     )
     over_plane(
-        lambda n, x: remote(rside, recv1s.at[rows8(16 * n0, 16)], pair(9), plane_id(n)).start()
+        lambda n, x: remote(rside, recv1s.at[rows8(16 * n0, 16)], pair(8), plane_id(n)).start()
     )
 
     signal(near, column_id(column_index(z + 4, core)))
@@ -322,8 +322,9 @@
         return hi, lo
 
     packed_hi, packed_lo = lax.fori_loop(0, 16, pack, (zero_face, zero_face))
-    hy_out_hi[...] = packed_hi
-    hy_out_lo[...] = packed_lo
+    low = _iota((32, 128), 1) < 64
+    hy_out_hi[...] = jnp.where(low, packed_hi[:32], roll(packed_hi[32:], 64))
+    hy_out_lo[...] = jnp.where(low, roll(packed_lo[:32], 127), roll(packed_lo[32:], 63))
 
     x_up = (gx < 15, remote(hx_out_hi, hx_lo, (hsend.at[0], hrecv.at[0]), device + 32))
     x_dn = (gx > 0, remote(hx_out_lo, hx_hi, (hsend.at[1], hrecv.at[1]), device - 32))
@@ -346,11 +347,18 @@
         def _(copy=copy):
             copy.start()
 
+    pl.semaphore_wait(near, 2)
+    for at in (0, 7):
+
+        @pl.when(gy == at)
+        def _(at=at):
+            signal(cross, device + (12 if at == 0 else -12))
+
     for missing, ref in ((gx == 0, hx_lo), (gx == 15, hx_hi), (gy == 0, hy_lo), (gy == 7, hy_hi)):
 
         @pl.when(missing)
         def _(ref=ref):
-            ref[...] = zero_face
+            ref[...] = zero_face[: ref.shape[0]]
 
     for missing, start in ((gz == 0, 0), (gz == 3, 1088)):
 
@@ -369,15 +377,14 @@
     table1 = first_table(zh, n0)
     table_side = side_table(zh, n0)
     table_last = last_table(zh, n0)
-    table_side_last = side_last_table(gz)
-
-    pl.semaphore_wait(near, 2)
-
-    for at in (0, 7):
+    table_side_last = side_last_table(zh, gz)
+
+    for at, copy in ((3, y_up[1]), (4, y_dn[1])):
 
         @pl.when(gy == at)
-        def _(at=at):
-            signal(cross, device + (12 if at == 0 else -12))
+        def _(copy=copy):
+            pl.semaphore_wait(cross, 1)
+            copy.start()
 
     wait_bytes(recv1.at[pl.ds(0, 240)], rsem.at[0])
     first = first_stage(table1, recv1[...], roll)
@@ -386,17 +393,17 @@
     recv2[m0] = send2[m0]
     over_column(lambda m: remote(send2.at[m], recv2.at[m0], pair(1), column_id(m)).start())
 
-    @pl.when(jnp.logical_or(gy == 3, gy == 4))
-    def _():
-        pl.semaphore_wait(cross, 1)
-
-    for there, copy in faces[:4]:
+    inside = (
+        (jnp.logical_and(gy < 7, gy != 3), y_up[1]),
+        (jnp.logical_and(gy > 0, gy != 4), y_dn[1]),
+    ) + faces[2:4]
+    for there, copy in inside:
 
         @pl.when(there)
         def _(copy=copy):
             copy.start()
 
-    wait_bytes(recv1s.at[pl.ds(0, 240)], rsem.at[9])
+    wait_bytes(recv1s.at[pl.ds(0, 240)], rsem.at[8])
     data = jnp.concatenate([recv1s[64 * x : 64 * x + 64, :] for x in range(4)], 1)
     own, other = side_first(table_side, data, roll)
     for x in range(4):
@@ -429,15 +436,12 @@
         roll,
     )
     for cr in range(8):
-        here, there = lines[cr][:8], lines[cr][8:]
-        own3[pl.ds(cr, 8, stride=8), :] = jnp.where(zh == 0, here, there)
-        hop2[pl.ds(cr, 8, stride=8), :] = jnp.where(zh == 0, there, here)
-    remote(hop2, other3, pair(6), far).start()
-    recvs[rows8(32 * n0 + 16 * zh, 16), :] = own3[rows8(16 * xx, 16), :]
+        for h in range(2):
+            send6[h, pl.ds(cr, 8, stride=8), :] = lines[cr][8 * h : 8 * h + 8]
+    recv6[:, rows8(16 * n0, 16), :] = send6[:, rows8(16 * xx, 16), :]
     over_plane(
         lambda n, x: remote(
-            own3.at[rows8(16 * x, 16)],
-            recvs.at[rows8(32 * n0 + 16 * zh, 16)], pair(7), plane_id(n),
+            send6.at[:, rows8(16 * x, 16)], recv6.at[:, rows8(16 * n0, 16)], pair(6), plane_id(n)
         ).start()
     )
 
@@ -451,6 +455,9 @@
         def _(ref=ref, i=i):
             wait_bytes(ref, hrecv.at[i])
 
+    for ref, out in ((hy_lo, col_lo), (hy_hi, col_hi)):
+        out[0:32, :] = ref[...]
+        out[32:64, :] = roll(ref[...], 64)
     sub = _iota((64, 128), 0)
 
     def exchange(z, carry):
@@ -462,9 +469,9 @@
             center = slab(c, 0)
             below = jnp.where(sub == 0, hx_lo[pl.ds(at, 1), :], pltpu.roll(center, 1, 0))
             above = jnp.where(sub == 63, hx_hi[pl.ds(at, 1), :], pltpu.roll(center, 63, 0))
-            left = jnp.where(lane == 0, pltpu.roll(hy_lo[...], 128 - at, 1), pltpu.roll(center, 1, 1))
+            left = jnp.where(lane == 0, pltpu.roll(col_lo[...], 128 - at, 1), pltpu.roll(center, 1, 1))
             right = jnp.where(
-                lane == 127, pltpu.roll(hy_hi[...], 126 - at, 1), pltpu.roll(center, 127, 1)
+                lane == 127, pltpu.roll(col_hi[...], 127 - at, 1), pltpu.roll(center, 127, 1)
             )
             return center, (slab(c, -1), slab(c, 1), below, above, left, right)
 
@@ -479,15 +486,6 @@
         return carry
 
     lax.fori_loop(0, 16, exchange, 0)
-
-    wait_bytes(other3, rsem.at[6])
-    recvs[rows8(32 * n0 + 16 * (1 - zh), 16), :] = other3[rows8(16 * xx, 16), :]
-    over_plane(
-        lambda n, x: remote(
-            other3.at[rows8(16 * x, 16)],
-            recvs.at[rows8(32 * n0 + 16 * (1 - zh), 16)], pair(8), plane_id(n),
-        ).start()
-    )
 
     wait_bytes(recv3.at[pl.ds(0, 248)], rsem.at[2])
     folded = fold_stage([recv3[pl.ds(cr, 32, stride=8), :] for cr in range(8)], fold[...], roll)
@@ -501,24 +499,21 @@
         ).start()
     )
 
-    wait_bytes(recvs.at[pl.ds(0, 240)], rsem.at[7])
-    wait_bytes(recvs.at[pl.ds(0, 240)], rsem.at[8])
+    wait_bytes(recv6.at[:, pl.ds(0, 240)], rsem.at[6])
     columns = [
-        jnp.concatenate([recvs[pl.ds(8 * e + 4 * c + r, 32, stride=16), :] for r in range(4)], 0)
+        jnp.concatenate([recv6[h, pl.ds(8 * e + 4 * c + r, 16, stride=16), :] for r in range(4)], 0)
+        for h in (zh, 1 - zh)
         for c in range(2)
         for e in range(2)
     ]
     g = _mul(table_side_last, _right(jnp.concatenate(columns, 1)))
     low = _iota((16, 128), 1) < 64
-    for c in range(2):
-        halves = [
-            g[:16, 128 * q : 128 * q + 128] - roll(g[16:, 128 * q : 128 * q + 128], 64)
-            for q in (2 * c, 2 * c + 1)
-        ]
-        side = jnp.where(low, halves[0], roll(halves[1], 64))
-        for z in range(16):
-            rows = slice(64 * z, 64 * z + 64)
-            exch[c + 1, rows, :] = exch[c + 1, rows, :] + side[z : z + 1, :]
+    halves = [
+        g[:16, 128 * q : 128 * q + 128] - roll(g[16:, 128 * q : 128 * q + 128], 64) for q in range(8)
+    ]
+    sums = [jnp.where(low, halves[q], roll(halves[q + 1], 64)) for q in (0, 2, 4, 6)]
+    hop2[0:16, :], hop2[16:32, :] = sums[2], sums[3]
+    remote(hop2, other2, pair(7), far).start()
 
     wait_bytes(recv4.at[pl.ds(0, 240)], rsem.at[3])
     for a in range(2):
@@ -536,15 +531,21 @@
         ).start()
     )
 
+    wait_bytes(other2, rsem.at[7])
+    for c in range(2):
+        side = sums[c] + other2[16 * c : 16 * c + 16, :]
+        for at in range(16):
+            rows = slice(64 * at, 64 * at + 64)
+            exch[c + 1, rows, :] = exch[c + 1, rows, :] + side[at : at + 1, :]
+
     wait_bytes(recv1.at[pl.ds(0, 240)], ssem.at[0])
-    wait_bytes(recv1s.at[pl.ds(0, 240)], ssem.at[9])
+    wait_bytes(recv1s.at[pl.ds(0, 240)], ssem.at[8])
     wait_bytes(send2.at[pl.ds(0, 31)], ssem.at[1])
     wait_bytes(recv3.at[pl.ds(0, 248)], ssem.at[2])
     wait_bytes(recv4.at[pl.ds(0, 240)], ssem.at[3])
     wait_bytes(hop1, ssem.at[5])
-    wait_bytes(hop2, ssem.at[6])
-    wait_bytes(recvs.at[pl.ds(0, 240)], ssem.at[7])
-    wait_bytes(recvs.at[pl.ds(0, 240)], ssem.at[8])
+    wait_bytes(recv6.at[:, pl.ds(0, 240)], ssem.at[6])
+    wait_bytes(hop2, ssem.at[7])
     for there, copy in faces:
 
         @pl.when(there)
@@ -573,10 +574,10 @@
         buf(4, 1152, 128), buf(32, 64), buf(16, 128), *[pltpu.VMEM(t.shape, t.dtype) for t in tables], buf(2, 2, 2, 4, 2048), buf(256, 128), buf(256, 128),
         buf(16, 128), buf(256, 128), buf(256, 128), buf(32, 4, 128), buf(32, 4, 128),
         buf(128, 128), buf(256, 128), buf(256, 128), buf(256, 128), buf(32, 128), buf(128, 128),
-        buf(32, 128), buf(64, 128), buf(64, 128), buf(64, 128), buf(64, 128), buf(512, 128),
+        buf(32, 128), buf(64, 128), buf(2, 64, 128), buf(2, 256, 128), buf(32, 128), buf(32, 128),
         buf(64, 128), buf(64, 128), buf(64, 128), buf(64, 128),
-        buf(64, 128), buf(64, 128), buf(64, 128), buf(64, 128),
-        pltpu.SemaphoreType.DMA((13,)), pltpu.SemaphoreType.DMA((10,)), pltpu.SemaphoreType.DMA((10,)),
+        buf(32, 128), buf(32, 128), buf(32, 128), buf(32, 128), buf(64, 128), buf(64, 128),
+        pltpu.SemaphoreType.DMA((13,)), pltpu.SemaphoreType.DMA((9,)), pltpu.SemaphoreType.DMA((9,)),
         pltpu.SemaphoreType.DMA((6,)), pltpu.SemaphoreType.DMA((6,)),
         pltpu.SemaphoreType.REGULAR, pltpu.SemaphoreType.REGULAR,
     ]

time: 52.5 us -> 50.1 us (0.954)
  the two profiles are of different devices: /device:TPU:32 before, /device:TPU:1 now
where the time goes in v5:
time: 50.1 us; the launch traced here: 49.9 us
  Pallas kernels  48.5 us (97%)
  other arithmetic  1.35 us (3%)
    pallas_call x1, Pallas kernels, on_device(): pl.pallas_call(body, out_shape=[jax.ShapeDtypeStruct((3, 1024, 128), F32)...  48.5 us
    add x1, other arithmetic, on_device(): return exch.reshape(3, 16, 64, 128) + top.reshape(3, 1, 64, 128)  1.35 us

profile of v5, /device:TPU:1, one launch (start us, length us, event | category | flops | bytes accessed | tf_op | source)
XLA Modules:
  0.0 49.9 jit_solution(5379116328774140360)
XLA Ops:
  0.0 48.5 %adjoint.1 = (f32[3,1024,128]{2,1,0:T(8,128)S(1)}, f32[192,128]{1,0:T(8,128)S(1)}) custom-call(f32[3,1024,128]{2,1,0:T(8,128)} %bitcast.8, f32[1,1024,128]{2,1,0:T(8,128)} %bitcast.9, f32[32,64]{1,0:T(8,128)} %bitcast.10, f32[16,128]{1,0:T(8,128)} %bitcast.11, f32[2,2,4,2048]{3,2,1,0:T(4,128)} %ktop.1, f32[2,2,4,2048]{3,2,1,0:T(4,128)} %kside.1, ...), custom_call_target="tpu_custom_call" | custom-call | tf_op jit(solution)/shard_map/adjoint/pallas_call | solution.py:584
  48.5 1.4 %broadcast_add_fusion = f32[3,16,64,128]{3,2,1,0:T(8,128)} fusion(f32[3,16,64,128]{3,2,1,0:T(8,128)S(1)} %bitcast.6, f32[3,64,128]{2,1,0:T(8,128)S(1)} %bitcast.7), kind=kLoop, calls=%fused_computation | loop fusion | flops 393216 | bytes 3244032 | tf_op jit(solution)/shard_map/add | solution.py:606

commit v6 on v5

--- a/solution.py
+++ b/solution.py
@@ -445,48 +445,6 @@
         ).start()
     )
 
-    arrivals = (
-        (gx > 0, hx_lo, 0), (gx < 15, hx_hi, 1), (gy > 0, hy_lo, 2), (gy < 7, hy_hi, 3),
-        (gz > 0, field.at[:, pl.ds(0, 64)], 4), (gz < 3, field.at[:, pl.ds(1088, 64)], 5),
-    )
-    for there, ref, i in arrivals:
-
-        @pl.when(there)
-        def _(ref=ref, i=i):
-            wait_bytes(ref, hrecv.at[i])
-
-    for ref, out in ((hy_lo, col_lo), (hy_hi, col_hi)):
-        out[0:32, :] = ref[...]
-        out[32:64, :] = roll(ref[...], 64)
-    sub = _iota((64, 128), 0)
-
-    def exchange(z, carry):
-        def slab(c, step):
-            return field[c, rows8(64 + 64 * (z + step), 64), :]
-
-        def around(c):
-            at = 16 * c + z
-            center = slab(c, 0)
-            below = jnp.where(sub == 0, hx_lo[pl.ds(at, 1), :], pltpu.roll(center, 1, 0))
-            above = jnp.where(sub == 63, hx_hi[pl.ds(at, 1), :], pltpu.roll(center, 63, 0))
-            left = jnp.where(lane == 0, pltpu.roll(col_lo[...], 128 - at, 1), pltpu.roll(center, 1, 1))
-            right = jnp.where(
-                lane == 127, pltpu.roll(col_hi[...], 127 - at, 1), pltpu.roll(center, 127, 1)
-            )
-            return center, (slab(c, -1), slab(c, 1), below, above, left, right)
-
-        a, near = around(3)
-        weights = [4.0 * a * b / (a + b) for b in near]
-        for c in range(3):
-            m, beside = around(c)
-            total = weights[0] * (m - beside[0])
-            for w, b in zip(weights[1:], beside[1:]):
-                total = total + w * (m - b)
-            exch[c, rows8(64 * z, 64), :] = total
-        return carry
-
-    lax.fori_loop(0, 16, exchange, 0)
-
     wait_bytes(recv3.at[pl.ds(0, 248)], rsem.at[2])
     folded = fold_stage([recv3[pl.ds(cr, 32, stride=8), :] for cr in range(8)], fold[...], roll)
     for cr in range(8):
@@ -514,6 +472,48 @@
     sums = [jnp.where(low, halves[q], roll(halves[q + 1], 64)) for q in (0, 2, 4, 6)]
     hop2[0:16, :], hop2[16:32, :] = sums[2], sums[3]
     remote(hop2, other2, pair(7), far).start()
+
+    arrivals = (
+        (gx > 0, hx_lo, 0), (gx < 15, hx_hi, 1), (gy > 0, hy_lo, 2), (gy < 7, hy_hi, 3),
+        (gz > 0, field.at[:, pl.ds(0, 64)], 4), (gz < 3, field.at[:, pl.ds(1088, 64)], 5),
+    )
+    for there, ref, i in arrivals:
+
+        @pl.when(there)
+        def _(ref=ref, i=i):
+            wait_bytes(ref, hrecv.at[i])
+
+    for ref, out in ((hy_lo, col_lo), (hy_hi, col_hi)):
+        out[0:32, :] = ref[...]
+        out[32:64, :] = roll(ref[...], 64)
+    sub = _iota((64, 128), 0)
+
+    def exchange(z, carry):
+        def slab(c, step):
+            return field[c, rows8(64 + 64 * (z + step), 64), :]
+
+        def around(c):
+            at = 16 * c + z
+            center = slab(c, 0)
+            below = jnp.where(sub == 0, hx_lo[pl.ds(at, 1), :], pltpu.roll(center, 1, 0))
+            above = jnp.where(sub == 63, hx_hi[pl.ds(at, 1), :], pltpu.roll(center, 63, 0))
+            left = jnp.where(lane == 0, pltpu.roll(col_lo[...], 128 - at, 1), pltpu.roll(center, 1, 1))
+            right = jnp.where(
+                lane == 127, pltpu.roll(col_hi[...], 127 - at, 1), pltpu.roll(center, 127, 1)
+            )
+            return center, (slab(c, -1), slab(c, 1), below, above, left, right)
+
+        a, near = around(3)
+        weights = [4.0 * a * b / (a + b) for b in near]
+        for c in range(3):
+            m, beside = around(c)
+            total = weights[0] * (m - beside[0])
+            for w, b in zip(weights[1:], beside[1:]):
+                total = total + w * (m - b)
+            exch[c, rows8(64 * z, 64), :] = total
+        return carry
+
+    lax.fori_loop(0, 16, exchange, 0)
 
     wait_bytes(recv4.at[pl.ds(0, 240)], rsem.at[3])
     for a in range(2):

time: 50.1 us -> 50.1 us (level)
  no operation moved by 1% of the time
where the time goes in v6:
time: 50.1 us; the launch traced here: 49.9 us
  Pallas kernels  48.6 us (97%)
  other arithmetic  1.35 us (3%)
    pallas_call x1, Pallas kernels, on_device(): pl.pallas_call(body, out_shape=[jax.ShapeDtypeStruct((3, 1024, 128), F32)...  48.6 us
    add x1, other arithmetic, on_device(): return exch.reshape(3, 16, 64, 128) + top.reshape(3, 1, 64, 128)  1.35 us

profile of v6, /device:TPU:1, one launch (start us, length us, event | category | flops | bytes accessed | tf_op | source)
XLA Modules:
  0.0 49.9 jit_solution(14886278274610331028)
XLA Ops:
  0.0 48.6 %adjoint.1 = (f32[3,1024,128]{2,1,0:T(8,128)S(1)}, f32[192,128]{1,0:T(8,128)S(1)}) custom-call(f32[3,1024,128]{2,1,0:T(8,128)} %bitcast.8, f32[1,1024,128]{2,1,0:T(8,128)} %bitcast.9, f32[32,64]{1,0:T(8,128)} %bitcast.10, f32[16,128]{1,0:T(8,128)} %bitcast.11, f32[2,2,4,2048]{3,2,1,0:T(4,128)} %ktop.1, f32[2,2,4,2048]{3,2,1,0:T(4,128)} %kside.1, ...), custom_call_target="tpu_custom_call" | custom-call | tf_op jit(solution)/shard_map/adjoint/pallas_call | solution.py:584
  48.6 1.4 %broadcast_add_fusion = f32[3,16,64,128]{3,2,1,0:T(8,128)} fusion(f32[3,16,64,128]{3,2,1,0:T(8,128)S(1)} %bitcast.6, f32[3,64,128]{2,1,0:T(8,128)S(1)} %bitcast.7), kind=kLoop, calls=%fused_computation | loop fusion | flops 393216 | bytes 3244032 | tf_op jit(solution)/shard_map/add | solution.py:606

commit v7 on v6

--- a/solution.py
+++ b/solution.py
@@ -297,9 +297,6 @@
     over_plane(
         lambda n, x: remote(send1, recv1.at[rows8(16 * n0, 16)], pair(0), plane_id(n)).start()
     )
-    over_plane(
-        lambda n, x: remote(rside, recv1s.at[rows8(16 * n0, 16)], pair(8), plane_id(n)).start()
-    )
 
     signal(near, column_id(column_index(z + 4, core)))
     signal(near, column_id(column_index(z + 12, core)))
@@ -347,6 +344,10 @@
         def _(copy=copy):
             copy.start()
 
+    over_plane(
+        lambda n, x: remote(rside, recv1s.at[rows8(16 * n0, 16)], pair(8), plane_id(n)).start()
+    )
+
     pl.semaphore_wait(near, 2)
     for at in (0, 7):
 
@@ -378,13 +379,6 @@
     table_side = side_table(zh, n0)
     table_last = last_table(zh, n0)
     table_side_last = side_last_table(zh, gz)
-
-    for at, copy in ((3, y_up[1]), (4, y_dn[1])):
-
-        @pl.when(gy == at)
-        def _(copy=copy):
-            pl.semaphore_wait(cross, 1)
-            copy.start()
 
     wait_bytes(recv1.at[pl.ds(0, 240)], rsem.at[0])
     first = first_stage(table1, recv1[...], roll)
@@ -410,6 +404,13 @@
         line1[rows8(32 * zh + 8 * x, 8), :] = own[x]
         hop1[8 * x : 8 * x + 8, :] = other[x]
     remote(hop1, line1.at[rows8(32 * zh, 32)], pair(5), far).start()
+
+    for at, copy in ((3, y_up[1]), (4, y_dn[1])):
+
+        @pl.when(gy == at)
+        def _(copy=copy):
+            pl.semaphore_wait(cross, 1)
+            copy.start()
 
     wait_bytes(recv2.at[pl.ds(0, 31)], rsem.at[1])
     shared = (twist[...], fwd[...], inv[...], back[...])

time: 50.1 us -> 48.6 us (0.970)
  Pallas kernels: 48.6 us -> 47.1 us
    pallas_call x1, Pallas kernels: 48.6 us -> 47.1 us  [on_device(): pl.pallas_call(body, out_shape=[jax.ShapeDtypeStruct((3, 1024, 128), F32)...]
where the time goes in v7:
time: 48.6 us; the launch traced here: 48.4 us
  Pallas kernels  47.1 us (97%)
  other arithmetic  1.35 us (3%)
    pallas_call x1, Pallas kernels, on_device(): pl.pallas_call(body, out_shape=[jax.ShapeDtypeStruct((3, 1024, 128), F32)...  47.1 us
    add x1, other arithmetic, on_device(): return exch.reshape(3, 16, 64, 128) + top.reshape(3, 1, 64, 128)  1.35 us

profile of v7, /device:TPU:1, one launch (start us, length us, event | category | flops | bytes accessed | tf_op | source)
XLA Modules:
  0.0 48.4 jit_solution(12005523916059772107)
XLA Ops:
  0.0 47.1 %adjoint.1 = (f32[3,1024,128]{2,1,0:T(8,128)S(1)}, f32[192,128]{1,0:T(8,128)S(1)}) custom-call(f32[3,1024,128]{2,1,0:T(8,128)} %bitcast.8, f32[1,1024,128]{2,1,0:T(8,128)} %bitcast.9, f32[32,64]{1,0:T(8,128)} %bitcast.10, f32[16,128]{1,0:T(8,128)} %bitcast.11, f32[2,2,4,2048]{3,2,1,0:T(4,128)} %ktop.1, f32[2,2,4,2048]{3,2,1,0:T(4,128)} %kside.1, ...), custom_call_target="tpu_custom_call" | custom-call | tf_op jit(solution)/shard_map/adjoint/pallas_call | solution.py:585
  47.1 1.4 %broadcast_add_fusion = f32[3,16,64,128]{3,2,1,0:T(8,128)} fusion(f32[3,16,64,128]{3,2,1,0:T(8,128)S(1)} %bitcast.6, f32[3,64,128]{2,1,0:T(8,128)S(1)} %bitcast.7), kind=kLoop, calls=%fused_computation | loop fusion | flops 393216 | bytes 3244032 | tf_op jit(solution)/shard_map/add | solution.py:607

commit v8 on v7

--- a/solution.py
+++ b/solution.py
@@ -555,9 +555,27 @@
 
     wait_bytes(recv5.at[pl.ds(0, 120)], rsem.at[4])
     lines_y = jnp.concatenate([recv5[pl.ds(q, 16, stride=8), :] for q in range(8)], 0)
-    top[0:128, :] = lines_y.T
-    top[128:192, :] = zero_face
+    top[...] = lines_y.T
     wait_bytes(recv5.at[pl.ds(0, 120)], ssem.at[4])
+
+
+CHUNKS = 8
+
+
+def add_top(exch, top, out, total, sems):
+    size = 2048 // CHUNKS
+    copies = [pltpu.make_async_copy(exch.at[2], out.at[2], sems.at[CHUNKS])]
+    copies[0].start()
+    for k in range(CHUNKS):
+        c, start = divmod(k * size, 1024)
+        image = top[64 * c : 64 * c + 64, :]
+        for at in range(start, start + size, 64):
+            total[c, at : at + 64, :] = exch[c, at : at + 64, :] + image
+        rows = pl.ds(start, size)
+        copies.append(pltpu.make_async_copy(total.at[c, rows], out.at[c, rows], sems.at[k]))
+        copies[-1].start()
+    for copy in copies:
+        copy.wait()
 
 
 def on_device(magnetization, stiffness, residual_top, residual_side, top_kernel, side_kernel):
@@ -586,7 +604,7 @@
         body,
         out_shape=[
             jax.ShapeDtypeStruct((3, 1024, 128), F32),
-            jax.ShapeDtypeStruct((192, 128), F32),
+            jax.ShapeDtypeStruct((128, 128), F32),
         ],
         in_specs=[hbm] * (6 + len(tables)),
         out_specs=[vmem] * 2,
@@ -604,7 +622,16 @@
         pin(side_kernel),
         *[pin(t) for t in tables],
     )
-    return exch.reshape(3, 16, 64, 128) + top.reshape(3, 1, 64, 128)
+    out = pl.pallas_call(
+        add_top,
+        out_shape=jax.ShapeDtypeStruct((3, 1024, 128), F32),
+        in_specs=[vmem, vmem],
+        out_specs=hbm,
+        scratch_shapes=[buf(2, 1024, 128), pltpu.SemaphoreType.DMA((CHUNKS + 1,))],
+        compiler_params=pltpu.CompilerParams(vmem_limit_bytes=4 * 1024 * 1024),
+        name="add_top",
+    )(exch, top)
+    return out.reshape(3, 16, 64, 128)
 
 
 def solution(mesh):

time: 48.6 us -> 48.5 us (level)
  other arithmetic: 1.35 us -> 0 us
  Pallas kernels: 47.1 us -> 48.3 us
    add x1 -> x0, other arithmetic: 1.35 us -> none  [on_device(): return exch.reshape(3, 16, 64, 128) + top.reshape(3, 1, 64, 128)]
    pallas_call x0 -> x1, Pallas kernels: none -> 1.21 us  [on_device(): pl.pallas_call(add_top, out_shape=jax.ShapeDtypeStruct((3, 1024, 128), F3...]
where the time goes in v8:
time: 48.5 us; the launch traced here: 48.3 us
  Pallas kernels  48.3 us (100%)
    pallas_call x1, Pallas kernels, on_device(): pl.pallas_call(body, out_shape=[jax.ShapeDtypeStruct((3, 1024, 128), F32)...  47.1 us
    pallas_call x1, Pallas kernels, on_device(): pl.pallas_call(add_top, out_shape=jax.ShapeDtypeStruct((3, 1024, 128), F3...  1.21 us

profile of v8, /device:TPU:1, one launch (start us, length us, event | category | flops | bytes accessed | tf_op | source)
XLA Modules:
  0.0 48.3 jit_solution(2296910867748544879)
XLA Ops:
  0.0 47.1 %adjoint.1 = (f32[3,1024,128]{2,1,0:T(8,128)S(1)}, f32[128,128]{1,0:T(8,128)S(1)}) custom-call(f32[3,1024,128]{2,1,0:T(8,128)} %bitcast.5, f32[1,1024,128]{2,1,0:T(8,128)} %bitcast.6, f32[32,64]{1,0:T(8,128)} %bitcast.7, f32[16,128]{1,0:T(8,128)} %bitcast.8, f32[2,2,4,2048]{3,2,1,0:T(4,128)} %ktop.1, f32[2,2,4,2048]{3,2,1,0:T(4,128)} %kside.1, ...), custom_call_target="tpu_custom_call" | custom-call | tf_op jit(solution)/shard_map/adjoint/pallas_call | solution.py:603
  47.1 1.2 %add_top.1 = f32[3,1024,128]{2,1,0:T(8,128)} custom-call(f32[3,1024,128]{2,1,0:T(8,128)S(1)} %get-tuple-element.7.exch, f32[128,128]{1,0:T(8,128)S(1)} %get-tuple-element.8.top), custom_call_target="tpu_custom_call" | custom-call | tf_op jit(solution)/shard_map/add_top/pallas_call | solution.py:625

commit v9 on v8

--- a/solution.py
+++ b/solution.py
@@ -590,10 +590,10 @@
         return pltpu.VMEM(shape, F32)
 
     scratch = [
-        buf(4, 1152, 128), buf(32, 64), buf(16, 128), *[pltpu.VMEM(t.shape, t.dtype) for t in tables], buf(2, 2, 2, 4, 2048), buf(256, 128), buf(256, 128),
+        buf(4, 1152, 128), buf(32, 64), buf(16, 128), *[pltpu.VMEM(t.shape, t.dtype) for t in tables], buf(2, 2, 2, 4, 2048), buf(272, 128), buf(272, 128),
         buf(16, 128), buf(256, 128), buf(256, 128), buf(32, 4, 128), buf(32, 4, 128),
-        buf(128, 128), buf(256, 128), buf(256, 128), buf(256, 128), buf(32, 128), buf(128, 128),
-        buf(32, 128), buf(64, 128), buf(2, 64, 128), buf(2, 256, 128), buf(32, 128), buf(32, 128),
+        buf(136, 128), buf(264, 128), buf(272, 128), buf(272, 128), buf(40, 128), buf(136, 128),
+        buf(32, 128), buf(72, 128), buf(2, 72, 128), buf(2, 272, 128), buf(32, 128), buf(32, 128),
         buf(64, 128), buf(64, 128), buf(64, 128), buf(64, 128),
         buf(32, 128), buf(32, 128), buf(32, 128), buf(32, 128), buf(64, 128), buf(64, 128),
         pltpu.SemaphoreType.DMA((13,)), pltpu.SemaphoreType.DMA((9,)), pltpu.SemaphoreType.DMA((9,)),

time: 48.5 us -> 48.5 us (level)
  no operation moved by 1% of the time
where the time goes in v9:
time: 48.5 us; the launch traced here: 48.3 us
  Pallas kernels  48.3 us (100%)
    pallas_call x1, Pallas kernels, on_device(): pl.pallas_call(body, out_shape=[jax.ShapeDtypeStruct((3, 1024, 128), F32)...  47.1 us
    pallas_call x1, Pallas kernels, on_device(): pl.pallas_call(add_top, out_shape=jax.ShapeDtypeStruct((3, 1024, 128), F3...  1.21 us

profile of v9, /device:TPU:1, one launch (start us, length us, event | category | flops | bytes accessed | tf_op | source)
XLA Modules:
  0.0 48.3 jit_solution(5773300187219507692)
XLA Ops:
  0.0 47.1 %adjoint.1 = (f32[3,1024,128]{2,1,0:T(8,128)S(1)}, f32[128,128]{1,0:T(8,128)S(1)}) custom-call(f32[3,1024,128]{2,1,0:T(8,128)} %bitcast.5, f32[1,1024,128]{2,1,0:T(8,128)} %bitcast.6, f32[32,64]{1,0:T(8,128)} %bitcast.7, f32[16,128]{1,0:T(8,128)} %bitcast.8, f32[2,2,4,2048]{3,2,1,0:T(4,128)} %ktop.1, f32[2,2,4,2048]{3,2,1,0:T(4,128)} %kside.1, ...), custom_call_target="tpu_custom_call" | custom-call | tf_op jit(solution)/shard_map/adjoint/pallas_call | solution.py:603
  47.1 1.2 %add_top.1 = f32[3,1024,128]{2,1,0:T(8,128)} custom-call(f32[3,1024,128]{2,1,0:T(8,128)S(1)} %get-tuple-element.7.exch, f32[128,128]{1,0:T(8,128)S(1)} %get-tuple-element.8.top), custom_call_target="tpu_custom_call" | custom-call | tf_op jit(solution)/shard_map/add_top/pallas_call | solution.py:625
